TPU v7x, 32 devices: a whole 2x2x4 slice. The times are simulated.
32 devices in a mesh: seq: 16 (over z, x, core), head: 2 (over y).
Axes of the slice: x: 2, y: 2, z: 4, core: 2. Of those that a mesh axis runs over, the one named last changes fastest.
Arguments:
- queries: bfloat16 [6144, 32, 128], P(('seq', 'head')), may hold values from -6 to 6
- keys: bfloat16 [6144, 8, 128], P('seq', 'head'), may hold values from -6 to 6
- values: bfloat16 [6144, 8, 128], P('seq', 'head'), may hold values from -1.5 to 1.5
- outputs: bfloat16 [6144, 32, 128], P(('seq', 'head')), may hold values from -1.5 to 1.5
- output_gradient: bfloat16 [6144, 32, 128], P(('seq', 'head')), may hold values from -24 to 24
- lse: float32 [6144, 32], P(('seq', 'head')), may hold values from 5.5 to 7.5
Outputs:
- query_grad: bfloat16 [6144, 32, 128], P(('seq', 'head'))
- key_gradient: bfloat16 [6144, 8, 128], P('seq', 'head')
- value_gradient: bfloat16 [6144, 8, 128], P('seq', 'head')
All inputs are finite; a program needn't handle non-finite values.
Results may differ from a plain program's by a relative error of at most 0.0068.
Values may be sent and summed in bfloat16 or wider, within the bound.
No kernel may reach another device: no remote copies, remote signals or barrier semaphores. Data moves between devices by JAX's collectives and lax.ppermute only.
A program may use at most 64 MiB of HBM per device.

v0:
```python
import functools
import math

import jax
import jax.numpy as jnp
from jax import lax
from jax.experimental import pallas as pl
from jax.experimental.pallas import tpu as pltpu
from jax.sharding import PartitionSpec as P


LOG2E = math.log2(math.e)
F32 = jnp.float32
BF16 = jnp.bfloat16
ACROSS = ((1,), (1,))
INNER = ((1,), (0,))
DOWN = ((0,), (0,))
VMEM = pl.BlockSpec(memory_space=pltpu.VMEM)
SMEM = pl.BlockSpec(memory_space=pltpu.SMEM)
ANY = pl.BlockSpec(memory_space=pl.ANY)
HBM = pl.BlockSpec(memory_space=pltpu.HBM)


def turned(shard, axis, by):
    size = lax.axis_size(axis)
    return lax.ppermute(shard, axis, [(i, (i + by) % size) for i in range(size)])


def swapped(shard, axis):
    return lax.ppermute(shard, axis, [(i, i ^ 1) for i in range(lax.axis_size(axis))])


def dot(a, b, dims):
    return lax.dot_general(a, b, (dims, ((), ())), preferred_element_type=F32)


def params(mib):
    return pltpu.CompilerParams(vmem_limit_bytes=mib * 2**20)


def untangle(x):
    tokens, heads, dim = x.shape
    x = x.astype(F32).reshape(tokens // 2, 2, heads, dim)
    a, b = x[:, 0], x[:, 1]
    low = lax.broadcasted_iota(jnp.int32, a.shape, 1) < heads // 2
    first = jnp.where(low, a, pltpu.roll(b, heads // 2, axis=1))
    second = jnp.where(low, pltpu.roll(a, heads // 2, axis=1), b)
    return [y.reshape(-1, dim).astype(BF16) for y in (first, second)]


def tangle(first, second, tokens):
    rows, dim = first.shape
    heads = 2 * rows // tokens
    a, b = (y.astype(F32).reshape(tokens // 2, heads, dim) for y in (first, second))
    low = lax.broadcasted_iota(jnp.int32, a.shape, 1) < heads // 2
    even = jnp.where(low, a, pltpu.roll(b, heads // 2, axis=1))
    odd = jnp.where(low, pltpu.roll(a, heads // 2, axis=1), b)
    return jnp.stack([even, odd], 1).reshape(tokens, heads, dim).astype(BF16)


def first_kernel(heads, pair, side_ref, place_ref, q, g, q_out, g_out, sem):
    start = pl.multiple_of((1 - side_ref[0]) * heads, pair)
    parts = sem.shape[1]
    size = q.shape[0] // parts
    copies = []
    for n, (src, out) in enumerate(((q, q_out), (g, g_out))):
        for m in range(parts):
            here = pl.ds(m * size, size)
            view = src.at[here, pl.ds(start, pair), :]
            copies.append(pltpu.make_async_copy(view, out.at[here], sem.at[n, m]))
            copies[-1].start()
    for copy in copies:
        copy.wait()


def first(side, place, queries, gradient, heads, pair):
    tokens, _, dim = queries.shape
    return pl.pallas_call(
        functools.partial(first_kernel, heads, pair),
        in_specs=[SMEM, SMEM, HBM, HBM],
        out_specs=[VMEM] * 2,
        out_shape=[jax.ShapeDtypeStruct((tokens, pair, dim), BF16)] * 2,
        scratch_shapes=[pltpu.SemaphoreType.DMA((2, 4))],
        compiler_params=params(2),
        name="first",
    )(side, place, *(pltpu.with_memory_space_constraint(x, pltpu.HBM) for x in (queries, gradient)))


def rest_kernel(heads, pair, side_ref, q, g, *outs):
    outs = list(outs)
    count = heads // pair
    for i in range(1, count):
        start = pl.multiple_of((1 - side_ref[0]) * heads + i * pair, pair)
        rows = [untangle(src[:, pl.ds(start, pair), :]) for src in (q, g)]
        for j in range(2):
            out = outs.pop(0)
            for n in range(2):
                out[n] = rows[n][j]
    for i in range(count):
        start = pl.multiple_of(side_ref[0] * heads + i * pair, pair)
        for src in (q, g):
            out = outs.pop(0)
            out[0], out[1] = untangle(src[:, pl.ds(start, pair), :])


def rest(side, queries, gradient, heads, pair):
    tokens, _, dim = queries.shape
    count = heads // pair
    sizes = [2] * (2 * (count - 1)) + [2] * (2 * count)
    return pl.pallas_call(
        functools.partial(rest_kernel, heads, pair),
        in_specs=[SMEM, VMEM, VMEM],
        out_specs=[VMEM] * len(sizes),
        out_shape=[jax.ShapeDtypeStruct((n, tokens * pair // 2, dim), BF16) for n in sizes],
        compiler_params=params(4),
        name="rest",
    )(side, queries, gradient)


def split_kernel(k, v, whole, *refs):
    outs, (wide, buf, sem) = refs[:-3], refs[-3:]
    heads, length = whole.shape[1:3]
    groups = heads // len(outs)
    parts = sem.shape[1]
    size = k.shape[0] // parts
    copies = []
    for n, src in enumerate((k, v)):
        for m in range(parts):
            here = pl.ds(m * size, size)
            copies.append(pltpu.make_async_copy(src.at[here], buf.at[n, here], sem.at[n, m]))
            copies[-1].start()
    for n in range(2):
        for m in range(parts):
            copies[n * parts + m].wait()
        wide[...] = buf[n].astype(F32)
        for i in range(heads):
            x = wide[pl.ds(i, length, stride=heads), :].astype(BF16)
            whole[n, i] = x
            outs[i // groups][n, i % groups] = x


def split(keys, values, chunks):
    length, heads, dim = keys.shape
    sizes = [heads] + [heads // chunks] * chunks
    return pl.pallas_call(
        split_kernel,
        in_specs=[HBM, HBM],
        out_specs=[VMEM] * (1 + chunks),
        out_shape=[jax.ShapeDtypeStruct((2, n, length, dim), BF16) for n in sizes],
        scratch_shapes=[
            pltpu.VMEM((length * heads, dim), F32),
            pltpu.VMEM((2, length * heads, dim), BF16),
            pltpu.SemaphoreType.DMA((2, 2)),
        ],
        compiler_params=params(4),
        name="split",
    )(*(pltpu.with_memory_space_constraint(x.reshape(-1, dim), pltpu.HBM) for x in (keys, values)))


def parts_of(x, count):
    terms = []
    for _ in range(count):
        terms.append(x.astype(BF16))
        x = x - terms[-1].astype(F32)
    return terms


def stats_kernel(per, side_ref, g, o, lse, ours, other, rep, both):
    tokens, heads_all, dim = g.shape
    rows = tokens * per
    groups = heads_all // per
    lane = lax.broadcasted_iota(jnp.int32, (1, rows), 1)
    token = lax.broadcasted_iota(jnp.int32, (tokens, 1), 0)
    spread = (token == lane // per).astype(F32).astype(BF16)
    for n, term in enumerate(parts_of(lse[...] * LOG2E, 3)):
        part = dot(term, spread, INNER)
        if n == 0:
            rep[...] = part
        else:
            rep[...] += part
    for m in range(groups):
        line = rep[pl.ds(m * per, 1), :]
        for i in range(1, per):
            line = jnp.where(lane % per == i, rep[pl.ds(m * per + i, 1), :], line)
        both[0, pl.ds(m, 1), :] = line
    block = dim // per
    sub = lax.broadcasted_iota(jnp.int32, (1, 2 * per, dim), 1)
    cell = lax.broadcasted_iota(jnp.int32, (1, 2 * per, dim), 2)
    cell = jnp.where(cell % per == sub % per, cell // per, -1)
    which = lax.broadcasted_iota(jnp.int32, (block, 1, 1), 0)

    def tokens_block(t, carry):
        here = pl.ds(pl.multiple_of(t * block, block), block)
        line = pl.ds(pl.multiple_of(t * dim, dim), dim)
        for m in range(groups // 2):
            pick = pl.ds(2 * per * m, 2 * per)
            x = g[here, pick, :].astype(F32) * o[here, pick, :].astype(F32)
            x = jnp.sum(x, axis=-1, keepdims=True)
            x = jnp.sum(jnp.where(cell == which, x, 0.0), axis=0)
            for n in range(2):
                both[1, pl.ds(2 * m + n, 1), line] = jnp.sum(x[n * per : (n + 1) * per], axis=0, keepdims=True)
        return carry

    lax.fori_loop(0, tokens // block, tokens_block, 0)
    half = groups // 2
    side = side_ref[0]
    for n in range(2):
        low, high = both[n, pl.ds(0, half), :], both[n, pl.ds(half, half), :]
        ours[n] = jnp.where(side == 0, low, high)
        other[n] = jnp.where(side == 0, high, low)


def row_stats(side, gradient, outputs, lse, per):
    tokens, heads_all, _ = gradient.shape
    groups, rows = heads_all // per, tokens * per
    return pl.pallas_call(
        functools.partial(stats_kernel, per),
        in_specs=[SMEM, VMEM, VMEM, VMEM],
        out_specs=[VMEM, VMEM],
        out_shape=[jax.ShapeDtypeStruct((2, groups // 2, rows), F32)] * 2,
        scratch_shapes=[pltpu.VMEM((heads_all, rows), F32), pltpu.VMEM((2, groups, rows), F32)],
        compiler_params=params(8),
        name="row_stats",
    )(side, gradient, outputs, lse.T)


def join_kernel(where, blocks, place_ref, *refs):
    groups = len(where)
    here, came = refs[:groups], refs[groups:-3]
    outs, wide = refs[-3:-1], refs[-1]
    prev, back = came[: len(came) // 2], came[len(came) // 2 :]
    length = wide.shape[0] // groups
    even = place_ref[0] % 2 == 0
    inside = place_ref[0] < blocks - 2
    for n, out in enumerate(outs):
        for i, (m, at) in enumerate(where):
            total = here[i][n, pl.ds(2 * length, length), :]
            total += jnp.where(even, prev[m][n, at].astype(F32), 0.0)
            total += jnp.where(inside, back[m][n, at].astype(F32), 0.0)
            wide[pl.ds(i, length, stride=groups), :] = total
        out[...] = wide[...].astype(BF16)


def join(place, blocks, here, prev, back):
    groups = len(here)
    where = tuple((m, at) for m, x in enumerate(prev) for at in range(x.shape[1]))
    length, dim = prev[0].shape[2:]
    shape = (length * groups, dim)
    outs = pl.pallas_call(
        functools.partial(join_kernel, where, blocks),
        in_specs=[SMEM] + [VMEM] * (groups + 2 * len(prev)),
        out_specs=[VMEM] * 2,
        out_shape=[jax.ShapeDtypeStruct(shape, BF16)] * 2,
        scratch_shapes=[pltpu.VMEM(shape, F32)],
        compiler_params=params(4),
        name="join",
    )(place, *here, *prev, *back)
    return [x.reshape(length, groups, dim) for x in outs]


def merge_kernel(place_ref, *refs):
    here, prev, out = refs[:-2], refs[-2], refs[-1]
    length = prev.shape[2]
    odd = place_ref[0] % 2 == 1
    for n in range(2):
        for i, acc in enumerate(here):
            out[n, i] = (acc[n, pl.ds(0, length), :] + jnp.where(odd, prev[n, i].astype(F32), 0.0)).astype(BF16)


def merge(place, here, prev):
    return pl.pallas_call(
        merge_kernel,
        in_specs=[SMEM] + [VMEM] * (len(here) + 1),
        out_specs=VMEM,
        out_shape=jax.ShapeDtypeStruct(prev.shape, BF16),
        compiler_params=params(2),
        name="merge",
    )(place, *here, prev)


def place_kernel(plan, heads, side_ref, *refs):
    buf, sem = refs[-2:]
    out = refs[-3]
    tokens, pair = buf.shape[1:3]
    copies = []
    for m, (a, b, ours, first) in enumerate(plan):
        side = side_ref[0] if ours else 1 - side_ref[0]
        start = pl.multiple_of(side * heads + first, pair)
        buf[m] = tangle(refs[a[0]][a[1]], refs[b[0]][b[1]], tokens)
        copies.append(pltpu.make_async_copy(buf.at[m], out.at[:, pl.ds(start, pair), :], sem.at[m]))
        copies[-1].start()
    for copy in copies:
        copy.wait()


def place(side, pieces, plan, whole, shape, heads, pair):
    more = [] if whole is None else [whole]
    return pl.pallas_call(
        functools.partial(place_kernel, plan, heads),
        in_specs=[SMEM] + [VMEM] * len(pieces) + [ANY] * len(more),
        out_specs=ANY,
        out_shape=jax.ShapeDtypeStruct(shape, BF16),
        scratch_shapes=[
            pltpu.VMEM((len(plan), shape[0], pair, shape[2]), BF16),
            pltpu.SemaphoreType.DMA((len(plan),)),
        ],
        input_output_aliases={1 + len(pieces): 0} if more else {},
        compiler_params=params(4),
        name="place",
    )(side, *pieces, *more)


def attn_kernel(scale, spots, ours, add, side_ref, place_ref, q, g, stats, far, far_next, own_next, own, *refs):
    groups = len(spots)
    refs = list(refs[groups:] if add else refs)
    dq = refs.pop(0)
    accs = [refs.pop(0) for _ in range(groups)]
    kcat, vcat, qs, gs = refs[-4:]
    length = own.shape[2]
    rows, dim = dq.shape[1:]
    behind = 0 if ours else 1
    if q.shape[1] != rows:
        behind = 0
        for src, dst in ((q, qs), (g, gs)):
            dst[0], dst[1] = untangle(src[...])
        q, g = qs, gs
    place = place_ref[0]

    def fill(block, src, index, when):
        here = pl.ds(block * length, length)

        @pl.when(when)
        def _():
            for i, spot in enumerate(spots):
                kcat[i, here, :] = jnp.zeros((length, dim), BF16) if src is None else src[0, spot[index]]
                vcat[i, here, :] = jnp.zeros((length, dim), BF16) if src is None else src[1, spot[index]]

    fill(0, far, 2, place >= 2)
    fill(0, None, 2, place < 2)
    fill(1, own_next, 1, place % 2 == 1)
    fill(1, far_next, 2, jnp.logical_and(place % 2 == 0, place >= 2))
    fill(1, None, 2, place < 1)
    fill(2, own, 1, place >= 0)
    if not add:
        for acc in accs:
            acc[...] = jnp.zeros_like(acc)

    width = 256
    half = length // 2
    per = rows // half
    span = width // per
    window = 2 * length
    token = lax.broadcasted_iota(jnp.int32, (1, width), 1) // per
    key_id = lax.broadcasted_iota(jnp.int32, (span, 1), 0)
    side = side_ref[0] if ours else 1 - side_ref[0]
    off = pl.multiple_of(side * half, span)

    def operands(i, b):
        here = pl.ds(b * width, width)
        keys = pl.ds(pl.multiple_of(off + b * span, span), window + span)
        return q[spots[i][0], here, :], g[spots[i][0] + behind, here, :], keys, here

    def scores(i, b):
        qb, gb, keys, _ = operands(i, b)
        return dot(kcat[i, keys, :], qb, ACROSS), dot(vcat[i, keys, :], gb, ACROSS)

    def weights(i, b, s, dp):
        here = pl.ds(b * width, width)
        at = pl.ds(spots[i][1], 1)
        p = jnp.exp2(s * (scale * LOG2E) - stats[0, at, here])
        first = jnp.where(key_id > token, p[:span], 0.0)
        last = jnp.where(key_id <= token, p[window:], 0.0)
        p = jnp.concatenate([first, p[span:window], last], 0)
        ds = p * (dp - stats[1, at, here]) * scale
        return p.astype(BF16), ds.astype(BF16)

    steps = [(i, b) for i in range(groups) for b in range(rows // width)]
    ahead = scores(*steps[0])
    for m, (i, b) in enumerate(steps):
        now = ahead
        if m + 1 < len(steps):
            ahead = scores(*steps[m + 1])
        p, ds = weights(i, b, *now)
        qb, gb, keys, here = operands(i, b)
        accs[i][1, keys, :] += dot(p, gb, INNER)
        accs[i][0, keys, :] += dot(ds, qb, INNER)
        dq[i, here, :] = dot(ds, kcat[i, keys, :], DOWN).astype(BF16)
    if add:
        prev = refs[0]
        for n in range(2):
            for i in range(groups):
                prev[n, i] = accs[i][n, pl.ds(length, length), :].astype(BF16)


def attention(side, place, q, g, stats, kv, accs, spots, ours, scale):
    length, dim = kv[0].shape[2:]
    rows = stats.shape[2]
    groups = len(spots)
    add = accs is not None
    out_shape = [jax.ShapeDtypeStruct((groups, rows, dim), BF16)]
    out_shape += [jax.ShapeDtypeStruct((2, 3 * length, dim), F32)] * groups
    if add:
        out_shape += [jax.ShapeDtypeStruct((2, groups, length, dim), BF16)]
    operands = [q, g, stats, *kv] + list(accs or ())
    flops = 2 * 5 * groups * rows * (2 * length + 64) * dim
    return pl.pallas_call(
        functools.partial(attn_kernel, scale, spots, ours, add),
        in_specs=[SMEM, SMEM] + [VMEM] * len(operands),
        out_specs=[VMEM] * len(out_shape),
        out_shape=out_shape,
        scratch_shapes=[pltpu.VMEM((groups, 3 * length, dim), BF16)] * 2 + [pltpu.VMEM((2, rows, dim), BF16)] * 2,
        input_output_aliases={9 + i: 1 + i for i in range(groups)} if add else {},
        compiler_params=params(16),
        cost_estimate=pl.CostEstimate(flops=flops, bytes_accessed=0, transcendentals=0),
        name="attention",
    )(side, place, *operands)


def body(queries, keys, values, outputs, output_gradient, lse):
    _, heads_all, dim = queries.shape
    _, heads_kv, _ = keys.shape
    side = lax.axis_index("head")
    heads = heads_all // lax.axis_size("head")
    per = heads // heads_kv
    chunks = heads_kv // 2
    pair = 2 * per
    scale = dim ** (-0.5)
    side_s = side.astype(jnp.int32).reshape(1)
    place_s = lax.axis_index("seq").astype(jnp.int32).reshape(1)

    packed = first(side_s, place_s, queries, output_gradient, heads, pair)
    own_kv, *chunk_kv = split(keys, values, chunks)
    far_kv, far_next = [], []
    for i in range(chunks):
        far_kv.append(turned(chunk_kv[i], "seq", 2))
        far_next.append(swapped(far_kv[i], "seq"))
    own_next = swapped(own_kv, "seq")
    stats, stats_other = row_stats(side_s, output_gradient, outputs, lse, per)
    stats_got = swapped(stats_other, "head")
    others = rest(side_s, queries, output_gradient, heads, pair)
    mine_rows = others[2 * (chunks - 1) :]
    got = []
    got.append([swapped(packed[0], "head")])
    got[0].append(swapped(packed[1], "head"))
    for i, two in enumerate(others[: 2 * (chunks - 1)]):
        got.append([swapped(two, "head")] * 2)

    run = functools.partial(attention, side_s, place_s, scale=scale)
    ours, theirs, accs, prev_got, back_got = [], [], [], [], []
    count = 0
    for i in range(chunks):
        kv = (far_kv[i], far_next[i], own_next, own_kv)
        spots = tuple((j, 2 * i + j, j) for j in range(2))
        dq, *acc = run(*mine_rows[2 * i : 2 * i + 2], stats, kv, None, spots, True)
        ours.append(dq)
        for task in ((0, 1),) if i == 0 else ((0,), (1,)):
            spots = tuple((j if i == 0 else 0, 2 * i + j, j) for j in task)
            dq, *out, prev = run(*got[count], stats_got, kv, [acc[j] for j in task], spots, False)
            accs += out
            prev_got.append(swapped(prev, "seq"))
            theirs.append(swapped(dq, "head"))
            back_got.append(turned(merge(place_s, out, prev_got[-1]), "seq", -2))
            count += 1
    plan = [((i, 0), (i, 1), True, i * pair) for i in range(chunks)]
    plan += [((chunks, 0), (chunks, 1), False, 0)]
    plan += [((chunks + 2 * i - 1, 0), (chunks + 2 * i, 0), False, i * pair) for i in range(1, chunks - 1)]
    whole = place(side_s, ours + theirs[:-2], tuple(plan), None, queries.shape, heads, pair)
    plan = (((0, 0), (1, 0), False, (chunks - 1) * pair),)
    whole = place(side_s, theirs[-2:], plan, whole, queries.shape, heads, pair)
    return whole, *join(place_s, lax.axis_size("seq"), accs, prev_got, back_got)


def solution(mesh):
    assert mesh.shape["head"] == 2

    return jax.shard_map(
        body,
        mesh=mesh,
        in_specs=(
            P(("seq", "head"), None, None),
            P("seq", "head", None),
            P("seq", "head", None),
            P(("seq", "head"), None, None),
            P(("seq", "head"), None, None),
            P(("seq", "head"), None),
        ),
        out_specs=(P(("seq", "head"), None, None), P("seq", "head", None), P("seq", "head", None)),
        check_vma=False,
    )
```

profile of v0, /device:TPU:0, one launch (start us, length us, event | category | flops | bytes accessed | tf_op | source)
XLA Modules:
  0.0 80.9 jit_solution(15628698312072777849)
XLA Ops:
  0.6 1.4 %split.1 = (bf16[2,4,384,128]{3,2,1,0:T(8,128)(2,1)S(1)}, bf16[2,2,384,128]{3,2,1,0:T(8,128)(2,1)S(1)}, bf16[2,2,384,128]{3,2,1,0:T(8,128)(2,1)S(1)}) custom-call(bf16[1536,128]{1,0:T(8,128)(2,1)} %bitcast.8, bf16[1536,128]{1,0:T(8,128)(2,1)} %bitcast.9), custom_call_target="tpu_custom_call" | custom-call | tf_op jit(solution)/shard_map/split/pallas_call | solution.py:145
  2.0 0.6 collective-permute-start.4
  2.6 2.5 %collective-permute-start.8 = (bf16[2,2,384,128]{3,2,1,0:T(8,128)(2,1)S(1)}, bf16[2,2,384,128]{3,2,1,0:T(8,128)(2,1)S(1)}, u32[]{:S(2)}, u32[]{:S(2)}) collective-permute-start(bf16[2,2,384,128]{3,2,1,0:T(8,128)(2,1)S(1)} %get-tuple-element.48), channel_id=1, source_target_pairs={{0,4},{2,6},{4,8},{6,10},{8,12},{10,14},{12,16},{14,18},{16,20},{1... | collective-permute-start | bytes 1179656 | tf_op jit(solution)/shard_map/ppermute | solution.py:26
  5.1 1.5 %collective-permute-start.2 = (bf16[2,2,384,128]{3,2,1,0:T(8,128)(2,1)S(1)}, bf16[2,2,384,128]{3,2,1,0:T(8,128)(2,1)S(1)}, u32[]{:S(2)}, u32[]{:S(2)}) collective-permute-start(bf16[2,2,384,128]{3,2,1,0:T(8,128)(2,1)S(1)} %get-tuple-element.36), channel_id=1, source_target_pairs={{0,4},{2,6},{4,8},{6,10},{8,12},{10,14},{12,16},{14,18},{16,20},{1... | collective-permute-start | bytes 1179656 | tf_op jit(solution)/shard_map/ppermute | solution.py:26
  6.6 11.5 %collective-permute-done.8.far = bf16[2,2,384,128]{3,2,1,0:T(8,128)(2,1)S(1)} collective-permute-done((bf16[2,2,384,128]{3,2,1,0:T(8,128)(2,1)S(1)}, bf16[2,2,384,128]{3,2,1,0:T(8,128)(2,1)S(1)}, u32[]{:S(2)}, u32[]{:S(2)}) %collective-permute-start.8) | collective-permute-done | bytes 393248 | tf_op jit(solution)/shard_map/ppermute | solution.py:26
  18.1 0.0 collective-permute-start.9
  18.1 1.4 %first.1 = (bf16[192,8,128]{2,1,0:T(8,128)(2,1)S(1)}, bf16[192,8,128]{2,1,0:T(8,128)(2,1)S(1)}) custom-call(s32[1]{0:T(128)} %bitcast.side_ref, s32[1]{0:T(128)} %bitcast.1.place_ref, bf16[192,32,128]{2,1,0:T(8,128)(2,1)} %q.3, bf16[192,32,128]{2,1,0:T(8,128)(2,1)} %g.5), custom_call_target="tpu_custom_call" | custom-call | tf_op jit(solution)/shard_map/first/pallas_call | solution.py:78
  19.6 1.8 %collective-permute-start.10 = (bf16[192,8,128]{2,1,0:T(8,128)(2,1)S(1)}, bf16[192,8,128]{2,1,0:T(8,128)(2,1)S(1)}, u32[]{:S(2)}, u32[]{:S(2)}) collective-permute-start(bf16[192,8,128]{2,1,0:T(8,128)(2,1)S(1)} %get-tuple-element.51), channel_id=1, source_target_pairs={{0,1},{1,0},{2,3},{3,2},{4,5},{5,4},{6,7},{7,6},{8,9},{9,8},{10,11... | collective-permute-start | bytes 1179656 | tf_op jit(solution)/shard_map/ppermute | solution.py:30
  21.3 0.3 collective-permute-start.11
  21.7 0.7 rest.1
  22.4 0.4 copy-done.2
  22.7 1.7 %row_stats.1 = (f32[2,4,768]{2,1,0:T(4,128)S(1)}, f32[2,4,768]{2,1,0:T(4,128)S(1)}) custom-call(s32[1]{0:T(128)} %bitcast.side_ref, bf16[192,32,128]{2,1,0:T(8,128)(2,1)S(1)} %copy-done, bf16[192,32,128]{2,1,0:T(8,128)(2,1)S(1)} %copy-done.2, f32[32,192]{1,0:T(8,128)S(1)} %bitcast.7), custom_call_target="tpu_custom_call" | custom-call | tf_op jit(solution)/shard_map/row_stats/pallas_call | solution.py:216
  24.4 1.9 %collective-permute-done.2.far = bf16[2,2,384,128]{3,2,1,0:T(8,128)(2,1)S(1)} collective-permute-done((bf16[2,2,384,128]{3,2,1,0:T(8,128)(2,1)S(1)}, bf16[2,2,384,128]{3,2,1,0:T(8,128)(2,1)S(1)}, u32[]{:S(2)}, u32[]{:S(2)}) %collective-permute-start.2) | collective-permute-done | bytes 393248 | tf_op jit(solution)/shard_map/ppermute | solution.py:26
  26.3 1.5 %collective-permute-start.1 = (f32[2,4,768]{2,1,0:T(4,128)S(1)}, f32[2,4,768]{2,1,0:T(4,128)S(1)}, u32[]{:S(2)}, u32[]{:S(2)}) collective-permute-start(f32[2,4,768]{2,1,0:T(4,128)S(1)} %get-tuple-element.35), channel_id=1, source_target_pairs={{0,1},{1,0},{2,3},{3,2},{4,5},{5,4},{6,7},{7,6},{8,9},{9,8},{10,11... | collective-permute-start | bytes 73736 | tf_op jit(solution)/shard_map/ppermute | solution.py:30
  27.8 0.5 collective-permute-start.6
  28.3 0.0 collective-permute-done.9.far_next
  28.3 0.0 collective-permute-start.3
  28.3 3.9 %attention.8 = (bf16[2,768,128]{2,1,0:T(8,128)(2,1)S(1)}, f32[2,1152,128]{2,1,0:T(8,128)S(1)}, f32[2,1152,128]{2,1,0:T(8,128)S(1)}) custom-call(s32[1]{0:T(128)} %bitcast.side_ref, s32[1]{0:T(128)} %bitcast.1.place_ref, bf16[2,768,128]{2,1,0:T(8,128)(2,1)S(1)} %get-tuple-element.46.q, bf16[2,768,128]{2,1,0:T(8,128)(2,1)S(1)} %get-tuple-element.47.g, ...), custom_call_target="tpu_custom_call" | custom-call | flops 1635778560 | tf_op jit(solution)/shard_map/attention/pallas_call | solution.py:406
  32.2 8.4 %collective-permute-done.1.stats = f32[2,4,768]{2,1,0:T(4,128)S(1)} collective-permute-done((f32[2,4,768]{2,1,0:T(4,128)S(1)}, f32[2,4,768]{2,1,0:T(4,128)S(1)}, u32[]{:S(2)}, u32[]{:S(2)}) %collective-permute-start.1) | collective-permute-done | bytes 24608 | tf_op jit(solution)/shard_map/ppermute | solution.py:30
  40.6 1.7 %collective-permute-start = (bf16[2,768,128]{2,1,0:T(8,128)(2,1)S(1)}, bf16[2,768,128]{2,1,0:T(8,128)(2,1)S(1)}, u32[]{:S(2)}, u32[]{:S(2)}) collective-permute-start(bf16[2,768,128]{2,1,0:T(8,128)(2,1)S(1)} %get-tuple-element.34), channel_id=1, source_target_pairs={{0,1},{1,0},{2,3},{3,2},{4,5},{5,4},{6,7},{7,6},{8,9},{9,8},{10,11... | collective-permute-start | bytes 1179656 | tf_op jit(solution)/shard_map/ppermute | solution.py:30
  42.3 0.0 collective-permute-done.11.g
  42.3 3.9 %attention.9 = (bf16[2,768,128]{2,1,0:T(8,128)(2,1)S(1)}, f32[2,1152,128]{2,1,0:T(8,128)S(1)}, f32[2,1152,128]{2,1,0:T(8,128)S(1)}, bf16[2,2,384,128]{3,2,1,0:T(8,128)(2,1)S(1)}) custom-call(s32[1]{0:T(128)} %bitcast.side_ref, s32[1]{0:T(128)} %bitcast.1.place_ref, ...), custom_call_target="tpu_custom_call", output_to_operand_aliasing={{1}: (9, {}), {2}: (10, {})} | custom-call | flops 1635778560 | tf_op jit(solution)/shard_map/attention/pallas_call | solution.py:406
  46.2 0.1 collective-permute-start.13
  46.3 0.4 collective-permute-start.12
  46.7 4.1 %attention.5 = (bf16[2,768,128]{2,1,0:T(8,128)(2,1)S(1)}, f32[2,1152,128]{2,1,0:T(8,128)S(1)}, f32[2,1152,128]{2,1,0:T(8,128)S(1)}) custom-call(s32[1]{0:T(128)} %bitcast.side_ref, s32[1]{0:T(128)} %bitcast.1.place_ref, bf16[2,768,128]{2,1,0:T(8,128)(2,1)S(1)} %get-tuple-element.38.q, bf16[2,768,128]{2,1,0:T(8,128)(2,1)S(1)} %get-tuple-element.39.g, ...), custom_call_target="tpu_custom_call" | custom-call | flops 1635778560 | tf_op jit(solution)/shard_map/attention/pallas_call | solution.py:406
  50.8 2.0 %attention.7 = (bf16[1,768,128]{2,1,0:T(8,128)(2,1)S(1)}, f32[2,1152,128]{2,1,0:T(8,128)S(1)}, bf16[2,1,384,128]{3,2,1,0:T(8,128)(2,1)S(1)}) custom-call(s32[1]{0:T(128)} %bitcast.side_ref, s32[1]{0:T(128)} %bitcast.1.place_ref, bf16[2,768,128]{2,1,0:T(8,128)(2,1)S(1)} %collective-permute-done.6.q.g, ...), custom_call_target="tpu_custom_call", output_to_operand_aliasing={{1}: (9, {})} | custom-call | flops 817889280 | tf_op jit(solution)/shard_map/attention/pallas_call | solution.py:406
  52.7 0.2 collective-permute-start.15
  52.9 4.5 %collective-permute-done.q.g = bf16[2,768,128]{2,1,0:T(8,128)(2,1)S(1)} collective-permute-done((bf16[2,768,128]{2,1,0:T(8,128)(2,1)S(1)}, bf16[2,768,128]{2,1,0:T(8,128)(2,1)S(1)}, u32[]{:S(2)}, u32[]{:S(2)}) %collective-permute-start) | collective-permute-done | bytes 393248 | tf_op jit(solution)/shard_map/ppermute | solution.py:30
  57.4 1.9 %attention.6 = (bf16[1,768,128]{2,1,0:T(8,128)(2,1)S(1)}, f32[2,1152,128]{2,1,0:T(8,128)S(1)}, bf16[2,1,384,128]{3,2,1,0:T(8,128)(2,1)S(1)}) custom-call(s32[1]{0:T(128)} %bitcast.side_ref, s32[1]{0:T(128)} %bitcast.1.place_ref, bf16[2,768,128]{2,1,0:T(8,128)(2,1)S(1)} %collective-permute-done.q.g, ...), custom_call_target="tpu_custom_call", output_to_operand_aliasing={{1}: (9, {})} | custom-call | flops 817889280 | tf_op jit(solution)/shard_map/attention/pallas_call | solution.py:406
  59.4 0.1 collective-permute-start.14
  59.4 0.0 collective-permute-done.13.refs_2_.refs_4_
  59.4 0.1 merge.3
  59.6 2.0 %collective-permute-start.16 = (bf16[2,2,384,128]{3,2,1,0:T(8,128)(2,1)S(1)}, bf16[2,2,384,128]{3,2,1,0:T(8,128)(2,1)S(1)}, u32[]{:S(2)}, u32[]{:S(2)}) collective-permute-start(bf16[2,2,384,128]{3,2,1,0:T(8,128)(2,1)S(1)} %merge.3), channel_id=1, source_target_pairs={{0,28},{2,30},{4,0},{6,2},{8,4},{10,6},{12,8},{14,10},{16,12},{18,... | collective-permute-start | bytes 1179656 | tf_op jit(solution)/shard_map/ppermute | solution.py:26
  61.6 1.5 %collective-permute-start.7 = (bf16[1,768,128]{2,1,0:T(8,128)(2,1)S(1)}, bf16[1,768,128]{2,1,0:T(8,128)(2,1)S(1)}, u32[]{:S(2)}, u32[]{:S(2)}) collective-permute-start(bf16[1,768,128]{2,1,0:T(8,128)(2,1)S(1)} %get-tuple-element.45), channel_id=1, source_target_pairs={{0,1},{1,0},{2,3},{3,2},{4,5},{5,4},{6,7},{7,6},{8,9},{9,8},{10,11... | collective-permute-start | bytes 589832 | tf_op jit(solution)/shard_map/ppermute | solution.py:30
  63.1 0.0 collective-permute-done.15.refs_1_.refs_6_
  63.1 0.5 collective-permute-start.5
  63.6 0.1 merge.5
  63.7 1.5 %collective-permute-start.18 = (bf16[2,1,384,128]{3,2,1,0:T(8,128)(2,1)S(1)}, bf16[2,1,384,128]{3,2,1,0:T(8,128)(2,1)S(1)}, u32[]{:S(2)}, u32[]{:S(2)}) collective-permute-start(bf16[2,1,384,128]{3,2,1,0:T(8,128)(2,1)S(1)} %merge.5), channel_id=1, source_target_pairs={{0,28},{2,30},{4,0},{6,2},{8,4},{10,6},{12,8},{14,10},{16,12},{18,... | collective-permute-start | bytes 589832 | tf_op jit(solution)/shard_map/ppermute | solution.py:26
  65.2 0.1 merge.4
  65.2 0.6 collective-permute-done.12.refs_2_
  65.8 2.0 %collective-permute-start.17 = (bf16[2,1,384,128]{3,2,1,0:T(8,128)(2,1)S(1)}, bf16[2,1,384,128]{3,2,1,0:T(8,128)(2,1)S(1)}, u32[]{:S(2)}, u32[]{:S(2)}) collective-permute-start(bf16[2,1,384,128]{3,2,1,0:T(8,128)(2,1)S(1)} %merge.4), channel_id=1, source_target_pairs={{0,28},{2,30},{4,0},{6,2},{8,4},{10,6},{12,8},{14,10},{16,12},{18,... | collective-permute-start | bytes 589832 | tf_op jit(solution)/shard_map/ppermute | solution.py:26
  67.9 1.1 %place.2.refs_2_ = bf16[192,32,128]{2,1,0:T(8,128)(2,1)} custom-call(s32[1]{0:T(128)} %bitcast.side_ref, bf16[2,768,128]{2,1,0:T(8,128)(2,1)S(1)} %get-tuple-element.49.refs_0_, bf16[2,768,128]{2,1,0:T(8,128)(2,1)S(1)} %get-tuple-element.50.refs_1_, bf16[2,768,128]{2,1,0:T(8,128)(2,1)S(1)} %collective-permute-done.12.refs_2_), custom_call_target="tpu_custom_call" | custom-call | tf_op jit(solution)/shard_map/place/pallas_call | solution.py:298
  69.0 1.1 %collective-permute-done.7.refs_1_ = bf16[1,768,128]{2,1,0:T(8,128)(2,1)S(1)} collective-permute-done((bf16[1,768,128]{2,1,0:T(8,128)(2,1)S(1)}, bf16[1,768,128]{2,1,0:T(8,128)(2,1)S(1)}, u32[]{:S(2)}, u32[]{:S(2)}) %collective-permute-start.7) | collective-permute-done | bytes 196640 | tf_op jit(solution)/shard_map/ppermute | solution.py:30
  70.1 3.8 %collective-permute-done.5.refs_0_ = bf16[1,768,128]{2,1,0:T(8,128)(2,1)S(1)} collective-permute-done((bf16[1,768,128]{2,1,0:T(8,128)(2,1)S(1)}, bf16[1,768,128]{2,1,0:T(8,128)(2,1)S(1)}, u32[]{:S(2)}, u32[]{:S(2)}) %collective-permute-start.5) | collective-permute-done | bytes 196640 | tf_op jit(solution)/shard_map/ppermute | solution.py:30
  73.8 0.8 %place.3 = bf16[192,32,128]{2,1,0:T(8,128)(2,1)} custom-call(s32[1]{0:T(128)} %bitcast.side_ref, bf16[1,768,128]{2,1,0:T(8,128)(2,1)S(1)} %collective-permute-done.5.refs_0_, bf16[1,768,128]{2,1,0:T(8,128)(2,1)S(1)} %collective-permute-done.7.refs_1_, bf16[192,32,128]{2,1,0:T(8,128)(2,1)} %place.2.refs_2_), custom_call_target="tpu_custom_call", output_to_operand_aliasing={{}: (3, {})} | custom-call | tf_op jit(solution)/shard_map/place/pallas_call | solution.py:298
  74.7 1.1 %collective-permute-done.18.refs_9_ = bf16[2,1,384,128]{3,2,1,0:T(8,128)(2,1)S(1)} collective-permute-done((bf16[2,1,384,128]{3,2,1,0:T(8,128)(2,1)S(1)}, bf16[2,1,384,128]{3,2,1,0:T(8,128)(2,1)S(1)}, u32[]{:S(2)}, u32[]{:S(2)}) %collective-permute-start.18) | collective-permute-done | bytes 196640 | tf_op jit(solution)/shard_map/ppermute | solution.py:26
  75.8 3.7 %collective-permute-done.17.refs_8_ = bf16[2,1,384,128]{3,2,1,0:T(8,128)(2,1)S(1)} collective-permute-done((bf16[2,1,384,128]{3,2,1,0:T(8,128)(2,1)S(1)}, bf16[2,1,384,128]{3,2,1,0:T(8,128)(2,1)S(1)}, u32[]{:S(2)}, u32[]{:S(2)}) %collective-permute-start.17) | collective-permute-done | bytes 196640 | tf_op jit(solution)/shard_map/ppermute | solution.py:26
  79.5 1.3 %join.1 = (bf16[1536,128]{1,0:T(8,128)(2,1)}, bf16[1536,128]{1,0:T(8,128)(2,1)}) custom-call(s32[1]{0:T(128)} %bitcast.1.place_ref, f32[2,1152,128]{2,1,0:T(8,128)S(1)} %get-tuple-element.56.refs_0_, f32[2,1152,128]{2,1,0:T(8,128)S(1)} %get-tuple-element.57.refs_1_, f32[2,1152,128]{2,1,0:T(8,128)S(1)} %get-tuple-element.58.refs_0_.refs_2_, ...), custom_call_target="tpu_custom_call" | custom-call | tf_op jit(solution)/shard_map/join/pallas_call | solution.py:249
  (13 shorter events, 0.0 us)
Async XLA Ops:
  2.0 25.8 %collective-permute-start.4 = (bf16[2,4,384,128]{3,2,1,0:T(8,128)(2,1)S(1)}, bf16[2,4,384,128]{3,2,1,0:T(8,128)(2,1)S(1)}, u32[]{:S(2)}, u32[]{:S(2)}) collective-permute-start(bf16[2,4,384,128]{3,2,1,0:T(8,128)(2,1)S(1)} %get-tuple-element.37.own), channel_id=1, source_target_pairs={{0,2},{2,0},{4,6},{6,4},{8,10},{10,8},{12,14},{14,12},{16,18},{18,... | collective-permute-start | bytes 2359304 | tf_op jit(solution)/shard_map/ppermute | solution.py:30
  2.6 15.5 %collective-permute-start.8 = (bf16[2,2,384,128]{3,2,1,0:T(8,128)(2,1)S(1)}, bf16[2,2,384,128]{3,2,1,0:T(8,128)(2,1)S(1)}, u32[]{:S(2)}, u32[]{:S(2)}) collective-permute-start(bf16[2,2,384,128]{3,2,1,0:T(8,128)(2,1)S(1)} %get-tuple-element.48), channel_id=1, source_target_pairs={{0,4},{2,6},{4,8},{6,10},{8,12},{10,14},{12,16},{14,18},{16,20},{1... | collective-permute-start | bytes 1179656 | tf_op jit(solution)/shard_map/ppermute | solution.py:26
  5.1 21.2 %collective-permute-start.2 = (bf16[2,2,384,128]{3,2,1,0:T(8,128)(2,1)S(1)}, bf16[2,2,384,128]{3,2,1,0:T(8,128)(2,1)S(1)}, u32[]{:S(2)}, u32[]{:S(2)}) collective-permute-start(bf16[2,2,384,128]{3,2,1,0:T(8,128)(2,1)S(1)} %get-tuple-element.36), channel_id=1, source_target_pairs={{0,4},{2,6},{4,8},{6,10},{8,12},{10,14},{12,16},{14,18},{16,20},{1... | collective-permute-start | bytes 1179656 | tf_op jit(solution)/shard_map/ppermute | solution.py:26
  18.1 10.2 %collective-permute-start.9 = (bf16[2,2,384,128]{3,2,1,0:T(8,128)(2,1)S(1)}, bf16[2,2,384,128]{3,2,1,0:T(8,128)(2,1)S(1)}, u32[]{:S(2)}, u32[]{:S(2)}) collective-permute-start(bf16[2,2,384,128]{3,2,1,0:T(8,128)(2,1)S(1)} %collective-permute-done.8.far), channel_id=1, source_target_pairs={{0,2},{2,0},{4,6},{6,4},{8,10},{10,8},{12,14},{14,12},{16,18},{18,... | collective-permute-start | bytes 1179656 | tf_op jit(solution)/shard_map/ppermute | solution.py:30
  18.1 3.6 %copy-start = (bf16[192,32,128]{2,1,0:T(8,128)(2,1)S(1)}, bf16[192,32,128]{2,1,0:T(8,128)(2,1)}, u32[]{:S(2)}) copy-start(bf16[192,32,128]{2,1,0:T(8,128)(2,1)} %g.5) | copy-start | bytes 4718596
  18.1 3.6 %copy-start.1 = (bf16[192,32,128]{2,1,0:T(8,128)(2,1)S(1)}, bf16[192,32,128]{2,1,0:T(8,128)(2,1)}, u32[]{:S(2)}) copy-start(bf16[192,32,128]{2,1,0:T(8,128)(2,1)} %q.3) | copy-start | bytes 4718596
  19.6 22.7 %collective-permute-start.10 = (bf16[192,8,128]{2,1,0:T(8,128)(2,1)S(1)}, bf16[192,8,128]{2,1,0:T(8,128)(2,1)S(1)}, u32[]{:S(2)}, u32[]{:S(2)}) collective-permute-start(bf16[192,8,128]{2,1,0:T(8,128)(2,1)S(1)} %get-tuple-element.51), channel_id=1, source_target_pairs={{0,1},{1,0},{2,3},{3,2},{4,5},{5,4},{6,7},{7,6},{8,9},{9,8},{10,11... | collective-permute-start | bytes 1179656 | tf_op jit(solution)/shard_map/ppermute | solution.py:30
  21.3 1.4 %copy-start.2 = (bf16[192,32,128]{2,1,0:T(8,128)(2,1)S(1)}, bf16[192,32,128]{2,1,0:T(8,128)(2,1)}, u32[]{:S(2)}) copy-start(bf16[192,32,128]{2,1,0:T(8,128)(2,1)} %o.1) | copy-start | bytes 4718596
  21.3 1.4 %copy-start.3 = (f32[192,32]{0,1:T(8,128)S(1)}, f32[192,32]{0,1:T(8,128)}, u32[]{:S(2)}) copy-start(f32[192,32]{0,1:T(8,128)} %param.11) | copy-start | bytes 73732
  21.3 20.9 %collective-permute-start.11 = (bf16[192,8,128]{2,1,0:T(8,128)(2,1)S(1)}, bf16[192,8,128]{2,1,0:T(8,128)(2,1)S(1)}, u32[]{:S(2)}, u32[]{:S(2)}) collective-permute-start(bf16[192,8,128]{2,1,0:T(8,128)(2,1)S(1)} %get-tuple-element.52), channel_id=1, source_target_pairs={{0,1},{1,0},{2,3},{3,2},{4,5},{5,4},{6,7},{7,6},{8,9},{9,8},{10,11... | collective-permute-start | bytes 1179656 | tf_op jit(solution)/shard_map/ppermute | solution.py:30
  26.3 14.3 %collective-permute-start.1 = (f32[2,4,768]{2,1,0:T(4,128)S(1)}, f32[2,4,768]{2,1,0:T(4,128)S(1)}, u32[]{:S(2)}, u32[]{:S(2)}) collective-permute-start(f32[2,4,768]{2,1,0:T(4,128)S(1)} %get-tuple-element.35), channel_id=1, source_target_pairs={{0,1},{1,0},{2,3},{3,2},{4,5},{5,4},{6,7},{7,6},{8,9},{9,8},{10,11... | collective-permute-start | bytes 73736 | tf_op jit(solution)/shard_map/ppermute | solution.py:30
  27.8 23.0 %collective-permute-start.6 = (bf16[2,768,128]{2,1,0:T(8,128)(2,1)S(1)}, bf16[2,768,128]{2,1,0:T(8,128)(2,1)S(1)}, u32[]{:S(2)}, u32[]{:S(2)}) collective-permute-start(bf16[2,768,128]{2,1,0:T(8,128)(2,1)S(1)} %get-tuple-element.43), channel_id=1, source_target_pairs={{0,1},{1,0},{2,3},{3,2},{4,5},{5,4},{6,7},{7,6},{8,9},{9,8},{10,11... | collective-permute-start | bytes 1179656 | tf_op jit(solution)/shard_map/ppermute | solution.py:30
  28.3 18.4 %collective-permute-start.3 = (bf16[2,2,384,128]{3,2,1,0:T(8,128)(2,1)S(1)}, bf16[2,2,384,128]{3,2,1,0:T(8,128)(2,1)S(1)}, u32[]{:S(2)}, u32[]{:S(2)}) collective-permute-start(bf16[2,2,384,128]{3,2,1,0:T(8,128)(2,1)S(1)} %collective-permute-done.2.far), channel_id=1, source_target_pairs={{0,2},{2,0},{4,6},{6,4},{8,10},{10,8},{12,14},{14,12},{16,18},{18,... | collective-permute-start | bytes 1179656 | tf_op jit(solution)/shard_map/ppermute | solution.py:30
  40.6 16.9 %collective-permute-start = (bf16[2,768,128]{2,1,0:T(8,128)(2,1)S(1)}, bf16[2,768,128]{2,1,0:T(8,128)(2,1)S(1)}, u32[]{:S(2)}, u32[]{:S(2)}) collective-permute-start(bf16[2,768,128]{2,1,0:T(8,128)(2,1)S(1)} %get-tuple-element.34), channel_id=1, source_target_pairs={{0,1},{1,0},{2,3},{3,2},{4,5},{5,4},{6,7},{7,6},{8,9},{9,8},{10,11... | collective-permute-start | bytes 1179656 | tf_op jit(solution)/shard_map/ppermute | solution.py:30
  46.2 13.2 %collective-permute-start.13 = (bf16[2,2,384,128]{3,2,1,0:T(8,128)(2,1)S(1)}, bf16[2,2,384,128]{3,2,1,0:T(8,128)(2,1)S(1)}, u32[]{:S(2)}, u32[]{:S(2)}) collective-permute-start(bf16[2,2,384,128]{3,2,1,0:T(8,128)(2,1)S(1)} %get-tuple-element.60), channel_id=1, source_target_pairs={{0,2},{2,0},{4,6},{6,4},{8,10},{10,8},{12,14},{14,12},{16,18},{18,... | collective-permute-start | bytes 1179656 | tf_op jit(solution)/shard_map/ppermute | solution.py:30
  46.3 19.5 %collective-permute-start.12 = (bf16[2,768,128]{2,1,0:T(8,128)(2,1)S(1)}, bf16[2,768,128]{2,1,0:T(8,128)(2,1)S(1)}, u32[]{:S(2)}, u32[]{:S(2)}) collective-permute-start(bf16[2,768,128]{2,1,0:T(8,128)(2,1)S(1)} %get-tuple-element.55), channel_id=1, source_target_pairs={{0,1},{1,0},{2,3},{3,2},{4,5},{5,4},{6,7},{7,6},{8,9},{9,8},{10,11... | collective-permute-start | bytes 1179656 | tf_op jit(solution)/shard_map/ppermute | solution.py:30
  52.7 10.4 %collective-permute-start.15 = (bf16[2,1,384,128]{3,2,1,0:T(8,128)(2,1)S(1)}, bf16[2,1,384,128]{3,2,1,0:T(8,128)(2,1)S(1)}, u32[]{:S(2)}, u32[]{:S(2)}) collective-permute-start(bf16[2,1,384,128]{3,2,1,0:T(8,128)(2,1)S(1)} %get-tuple-element.62), channel_id=1, source_target_pairs={{0,2},{2,0},{4,6},{6,4},{8,10},{10,8},{12,14},{14,12},{16,18},{18,... | collective-permute-start | bytes 589832 | tf_op jit(solution)/shard_map/ppermute | solution.py:30
  59.4 4.3 %collective-permute-start.14 = (bf16[2,1,384,128]{3,2,1,0:T(8,128)(2,1)S(1)}, bf16[2,1,384,128]{3,2,1,0:T(8,128)(2,1)S(1)}, u32[]{:S(2)}, u32[]{:S(2)}) collective-permute-start(bf16[2,1,384,128]{3,2,1,0:T(8,128)(2,1)S(1)} %get-tuple-element.61), channel_id=1, source_target_pairs={{0,2},{2,0},{4,6},{6,4},{8,10},{10,8},{12,14},{14,12},{16,18},{18,... | collective-permute-start | bytes 589832 | tf_op jit(solution)/shard_map/ppermute | solution.py:30
  59.6 20.0 %collective-permute-start.16 = (bf16[2,2,384,128]{3,2,1,0:T(8,128)(2,1)S(1)}, bf16[2,2,384,128]{3,2,1,0:T(8,128)(2,1)S(1)}, u32[]{:S(2)}, u32[]{:S(2)}) collective-permute-start(bf16[2,2,384,128]{3,2,1,0:T(8,128)(2,1)S(1)} %merge.3), channel_id=1, source_target_pairs={{0,28},{2,30},{4,0},{6,2},{8,4},{10,6},{12,8},{14,10},{16,12},{18,... | collective-permute-start | bytes 1179656 | tf_op jit(solution)/shard_map/ppermute | solution.py:26
  61.6 8.4 %collective-permute-start.7 = (bf16[1,768,128]{2,1,0:T(8,128)(2,1)S(1)}, bf16[1,768,128]{2,1,0:T(8,128)(2,1)S(1)}, u32[]{:S(2)}, u32[]{:S(2)}) collective-permute-start(bf16[1,768,128]{2,1,0:T(8,128)(2,1)S(1)} %get-tuple-element.45), channel_id=1, source_target_pairs={{0,1},{1,0},{2,3},{3,2},{4,5},{5,4},{6,7},{7,6},{8,9},{9,8},{10,11... | collective-permute-start | bytes 589832 | tf_op jit(solution)/shard_map/ppermute | solution.py:30
  63.1 10.7 %collective-permute-start.5 = (bf16[1,768,128]{2,1,0:T(8,128)(2,1)S(1)}, bf16[1,768,128]{2,1,0:T(8,128)(2,1)S(1)}, u32[]{:S(2)}, u32[]{:S(2)}) collective-permute-start(bf16[1,768,128]{2,1,0:T(8,128)(2,1)S(1)} %get-tuple-element.42), channel_id=1, source_target_pairs={{0,1},{1,0},{2,3},{3,2},{4,5},{5,4},{6,7},{7,6},{8,9},{9,8},{10,11... | collective-permute-start | bytes 589832 | tf_op jit(solution)/shard_map/ppermute | solution.py:30
  63.7 12.1 %collective-permute-start.18 = (bf16[2,1,384,128]{3,2,1,0:T(8,128)(2,1)S(1)}, bf16[2,1,384,128]{3,2,1,0:T(8,128)(2,1)S(1)}, u32[]{:S(2)}, u32[]{:S(2)}) collective-permute-start(bf16[2,1,384,128]{3,2,1,0:T(8,128)(2,1)S(1)} %merge.5), channel_id=1, source_target_pairs={{0,28},{2,30},{4,0},{6,2},{8,4},{10,6},{12,8},{14,10},{16,12},{18,... | collective-permute-start | bytes 589832 | tf_op jit(solution)/shard_map/ppermute | solution.py:26
  65.8 13.7 %collective-permute-start.17 = (bf16[2,1,384,128]{3,2,1,0:T(8,128)(2,1)S(1)}, bf16[2,1,384,128]{3,2,1,0:T(8,128)(2,1)S(1)}, u32[]{:S(2)}, u32[]{:S(2)}) collective-permute-start(bf16[2,1,384,128]{3,2,1,0:T(8,128)(2,1)S(1)} %merge.4), channel_id=1, source_target_pairs={{0,28},{2,30},{4,0},{6,2},{8,4},{10,6},{12,8},{14,10},{16,12},{18,... | collective-permute-start | bytes 589832 | tf_op jit(solution)/shard_map/ppermute | solution.py:26
where the time goes:
time: 81 us; the launch traced here: 80.9 us
  waiting for transfers between devices  36.5 us (45%)
  Pallas kernels  24.5 us (30%)
  starting transfers between devices  18.8 us (23%)
    ppermute x14, waiting for transfers between devices, swapped(): lax.ppermute(shard, axis, [(i, i ^ 1) for i in range(lax.axis_size(axis))])  18.3 us
    ppermute x5, waiting for transfers between devices, turned(): lax.ppermute(shard, axis, [(i, (i + by) % size) for i in range(size)])  18.2 us
    pallas_call x5, Pallas kernels, attention(): pl.pallas_call(functools.partial(attn_kernel, scale, spots, ours, add), i...  15.8 us
    ppermute x5, starting transfers between devices, turned(): lax.ppermute(shard, axis, [(i, (i + by) % size) for i in range(size)])  9.64 us
    ppermute x14, starting transfers between devices, swapped(): lax.ppermute(shard, axis, [(i, i ^ 1) for i in range(lax.axis_size(axis))])  9.11 us
    pallas_call x2, Pallas kernels, place(): pl.pallas_call(functools.partial(place_kernel, plan, heads), in_specs=[SM...  1.97 us
    pallas_call x1, Pallas kernels, row_stats(): pl.pallas_call(functools.partial(stats_kernel, per), in_specs=[SMEM, VMEM...  1.66 us
  transfers between devices with their start and end apart: 19, of which 9 were waited for; matrix products, arithmetic and copies ran while one was open for 0% of the time, Pallas kernels for 27%

commit v1 on v0

--- a/solution.py
+++ b/solution.py
@@ -58,32 +58,30 @@
     return jnp.stack([even, odd], 1).reshape(tokens, heads, dim).astype(BF16)
 
 
-def first_kernel(heads, pair, side_ref, place_ref, q, g, q_out, g_out, sem):
+def first_kernel(heads, pair, side_ref, place_ref, src, out, sem):
     start = pl.multiple_of((1 - side_ref[0]) * heads, pair)
-    parts = sem.shape[1]
-    size = q.shape[0] // parts
+    parts = sem.shape[0]
+    size = src.shape[0] // parts
     copies = []
-    for n, (src, out) in enumerate(((q, q_out), (g, g_out))):
-        for m in range(parts):
-            here = pl.ds(m * size, size)
-            view = src.at[here, pl.ds(start, pair), :]
-            copies.append(pltpu.make_async_copy(view, out.at[here], sem.at[n, m]))
-            copies[-1].start()
+    for m in range(parts):
+        here = pl.ds(m * size, size)
+        copies.append(pltpu.make_async_copy(src.at[here, pl.ds(start, pair), :], out.at[here], sem.at[m]))
+        copies[-1].start()
     for copy in copies:
         copy.wait()
 
 
-def first(side, place, queries, gradient, heads, pair):
-    tokens, _, dim = queries.shape
+def first(side, place, x, heads, pair):
+    tokens, _, dim = x.shape
     return pl.pallas_call(
         functools.partial(first_kernel, heads, pair),
-        in_specs=[SMEM, SMEM, HBM, HBM],
-        out_specs=[VMEM] * 2,
-        out_shape=[jax.ShapeDtypeStruct((tokens, pair, dim), BF16)] * 2,
-        scratch_shapes=[pltpu.SemaphoreType.DMA((2, 4))],
+        in_specs=[SMEM, SMEM, HBM],
+        out_specs=VMEM,
+        out_shape=jax.ShapeDtypeStruct((tokens, pair, dim), BF16),
+        scratch_shapes=[pltpu.SemaphoreType.DMA((4,))],
         compiler_params=params(2),
         name="first",
-    )(side, place, *(pltpu.with_memory_space_constraint(x, pltpu.HBM) for x in (queries, gradient)))
+    )(side, place, pltpu.with_memory_space_constraint(x, pltpu.HBM))
 
 
 def rest_kernel(heads, pair, side_ref, q, g, *outs):
@@ -224,38 +222,59 @@
     )(side, gradient, outputs, lse.T)
 
 
-def join_kernel(where, blocks, place_ref, *refs):
+def gather_kernel(where, blocks, place_ref, *refs):
     groups = len(where)
-    here, came = refs[:groups], refs[groups:-3]
-    outs, wide = refs[-3:-1], refs[-1]
-    prev, back = came[: len(came) // 2], came[len(came) // 2 :]
-    length = wide.shape[0] // groups
+    here, came, outs = refs[:groups], refs[groups:-2], refs[-2:]
+    prev, back = came[: len(came) // 2 + 1], came[len(came) // 2 + 1 :]
+    length = outs[0].shape[0] // groups
     even = place_ref[0] % 2 == 0
     inside = place_ref[0] < blocks - 2
     for n, out in enumerate(outs):
         for i, (m, at) in enumerate(where):
             total = here[i][n, pl.ds(2 * length, length), :]
             total += jnp.where(even, prev[m][n, at].astype(F32), 0.0)
-            total += jnp.where(inside, back[m][n, at].astype(F32), 0.0)
-            wide[pl.ds(i, length, stride=groups), :] = total
-        out[...] = wide[...].astype(BF16)
-
-
-def join(place, blocks, here, prev, back):
+            if m < len(back):
+                total += jnp.where(inside, back[m][n, at].astype(F32), 0.0)
+            out[pl.ds(i, length, stride=groups), :] = total
+
+
+def gather(place, blocks, here, prev, back):
     groups = len(here)
     where = tuple((m, at) for m, x in enumerate(prev) for at in range(x.shape[1]))
     length, dim = prev[0].shape[2:]
-    shape = (length * groups, dim)
+    return pl.pallas_call(
+        functools.partial(gather_kernel, where, blocks),
+        in_specs=[SMEM] + [VMEM] * (groups + len(prev) + len(back)),
+        out_specs=[VMEM] * 2,
+        out_shape=[jax.ShapeDtypeStruct((length * groups, dim), F32)] * 2,
+        compiler_params=params(2),
+        name="gather",
+    )(place, *here, *prev, *back)
+
+
+def join_kernel(blocks, place_ref, last, wide_k, wide_v, out_k, out_v, sum_k, sum_v):
+    length = last.shape[2]
+    groups = wide_k.shape[0] // length
+    inside = place_ref[0] < blocks - 2
+    for n, (out, total) in enumerate(((out_k, sum_k), (out_v, sum_v))):
+        rows = pl.ds(groups - 1, length, stride=groups)
+        total[rows, :] = total[rows, :] + jnp.where(inside, last[n, 0].astype(F32), 0.0)
+        out[...] = total[...].astype(BF16)
+
+
+def join(place, blocks, last, wide):
+    shape = wide[0].shape
+    length, dim = last.shape[2:]
     outs = pl.pallas_call(
-        functools.partial(join_kernel, where, blocks),
-        in_specs=[SMEM] + [VMEM] * (groups + 2 * len(prev)),
-        out_specs=[VMEM] * 2,
-        out_shape=[jax.ShapeDtypeStruct(shape, BF16)] * 2,
-        scratch_shapes=[pltpu.VMEM(shape, F32)],
-        compiler_params=params(4),
+        functools.partial(join_kernel, blocks),
+        in_specs=[SMEM] + [VMEM] * 3,
+        out_specs=[VMEM] * 4,
+        out_shape=[jax.ShapeDtypeStruct(shape, t) for t in (BF16, BF16, F32, F32)],
+        input_output_aliases={2: 2, 3: 3},
+        compiler_params=params(2),
         name="join",
-    )(place, *here, *prev, *back)
-    return [x.reshape(length, groups, dim) for x in outs]
+    )(place, last, *wide)
+    return [x.reshape(length, shape[0] // length, dim) for x in outs[:2]]
 
 
 def merge_kernel(place_ref, *refs):
@@ -428,7 +447,8 @@
     side_s = side.astype(jnp.int32).reshape(1)
     place_s = lax.axis_index("seq").astype(jnp.int32).reshape(1)
 
-    packed = first(side_s, place_s, queries, output_gradient, heads, pair)
+    packed = [first(side_s, place_s, queries, heads, pair)]
+    packed.append(first(side_s, place_s, output_gradient, heads, pair))
     own_kv, *chunk_kv = split(keys, values, chunks)
     far_kv, far_next = [], []
     for i in range(chunks):
@@ -467,7 +487,8 @@
     whole = place(side_s, ours + theirs[:-2], tuple(plan), None, queries.shape, heads, pair)
     plan = (((0, 0), (1, 0), False, (chunks - 1) * pair),)
     whole = place(side_s, theirs[-2:], plan, whole, queries.shape, heads, pair)
-    return whole, *join(place_s, lax.axis_size("seq"), accs, prev_got, back_got)
+    wide = gather(place_s, lax.axis_size("seq"), accs, prev_got, back_got[:-1])
+    return whole, *join(place_s, lax.axis_size("seq"), back_got[-1], wide)
 
 
 def solution(mesh):

time: 81 us -> 80.6 us (level)
  waiting for transfers between devices: 36.5 us -> 35.1 us
    ppermute x5, waiting for transfers between devices: 18.2 us -> 17.1 us  [turned(): lax.ppermute(shard, axis, [(i, (i + by) % size) for i in range(size)])]
    pallas_call x1 -> x2, Pallas kernels: 1.45 us -> 2.27 us  [first(): pl.pallas_call(functools.partial(first_kernel, heads, pair), in_specs=[SM...]
  transfers between devices with their start and end apart: 19 -> 19, of which waited for: 9 -> 9; matrix products, arithmetic and copies ran while one was open for 0% -> 0% of each run, Pallas kernels for 27% -> 29%
where the time goes in v1:
time: 80.6 us; the launch traced here: 80.3 us
  waiting for transfers between devices  35.1 us (44%)
  Pallas kernels  25.3 us (31%)
  starting transfers between devices  18.9 us (23%)
  between operations  0.82 us (1%)
    ppermute x14, waiting for transfers between devices, swapped(): lax.ppermute(shard, axis, [(i, i ^ 1) for i in range(lax.axis_size(axis))])  18.1 us
    ppermute x5, waiting for transfers between devices, turned(): lax.ppermute(shard, axis, [(i, (i + by) % size) for i in range(size)])  17.1 us
    pallas_call x5, Pallas kernels, attention(): pl.pallas_call(functools.partial(attn_kernel, scale, spots, ours, add), i...  15.8 us
    ppermute x5, starting transfers between devices, turned(): lax.ppermute(shard, axis, [(i, (i + by) % size) for i in range(size)])  9.64 us
    ppermute x14, starting transfers between devices, swapped(): lax.ppermute(shard, axis, [(i, i ^ 1) for i in range(lax.axis_size(axis))])  9.25 us
    pallas_call x2, Pallas kernels, first(): pl.pallas_call(functools.partial(first_kernel, heads, pair), in_specs=[SM...  2.27 us
    pallas_call x2, Pallas kernels, place(): pl.pallas_call(functools.partial(place_kernel, plan, heads), in_specs=[SM...  1.97 us
    pallas_call x1, Pallas kernels, row_stats(): pl.pallas_call(functools.partial(stats_kernel, per), in_specs=[SMEM, VMEM...  1.66 us
  transfers between devices with their start and end apart: 19, of which 9 were waited for; matrix products, arithmetic and copies ran while one was open for 0% of the time, Pallas kernels for 29%

profile of v1, /device:TPU:0, one launch (start us, length us, event | category | flops | bytes accessed | tf_op | source)
XLA Modules:
  0.0 80.3 jit_solution(6327283465420267457)
XLA Ops:
  0.6 1.4 %split.1 = (bf16[2,4,384,128]{3,2,1,0:T(8,128)(2,1)S(1)}, bf16[2,2,384,128]{3,2,1,0:T(8,128)(2,1)S(1)}, bf16[2,2,384,128]{3,2,1,0:T(8,128)(2,1)S(1)}) custom-call(bf16[1536,128]{1,0:T(8,128)(2,1)} %bitcast.8, bf16[1536,128]{1,0:T(8,128)(2,1)} %bitcast.9), custom_call_target="tpu_custom_call" | custom-call | tf_op jit(solution)/shard_map/split/pallas_call | solution.py:143
  2.0 0.6 collective-permute-start.4
  2.6 2.5 %collective-permute-start.8 = (bf16[2,2,384,128]{3,2,1,0:T(8,128)(2,1)S(1)}, bf16[2,2,384,128]{3,2,1,0:T(8,128)(2,1)S(1)}, u32[]{:S(2)}, u32[]{:S(2)}) collective-permute-start(bf16[2,2,384,128]{3,2,1,0:T(8,128)(2,1)S(1)} %get-tuple-element.48), channel_id=1, source_target_pairs={{0,4},{2,6},{4,8},{6,10},{8,12},{10,14},{12,16},{14,18},{16,20},{1... | collective-permute-start | bytes 1179656 | tf_op jit(solution)/shard_map/ppermute | solution.py:26
  5.1 1.5 %collective-permute-start.2 = (bf16[2,2,384,128]{3,2,1,0:T(8,128)(2,1)S(1)}, bf16[2,2,384,128]{3,2,1,0:T(8,128)(2,1)S(1)}, u32[]{:S(2)}, u32[]{:S(2)}) collective-permute-start(bf16[2,2,384,128]{3,2,1,0:T(8,128)(2,1)S(1)} %get-tuple-element.36), channel_id=1, source_target_pairs={{0,4},{2,6},{4,8},{6,10},{8,12},{10,14},{12,16},{14,18},{16,20},{1... | collective-permute-start | bytes 1179656 | tf_op jit(solution)/shard_map/ppermute | solution.py:26
  6.6 11.5 %collective-permute-done.8.far = bf16[2,2,384,128]{3,2,1,0:T(8,128)(2,1)S(1)} collective-permute-done((bf16[2,2,384,128]{3,2,1,0:T(8,128)(2,1)S(1)}, bf16[2,2,384,128]{3,2,1,0:T(8,128)(2,1)S(1)}, u32[]{:S(2)}, u32[]{:S(2)}) %collective-permute-start.8) | collective-permute-done | bytes 393248 | tf_op jit(solution)/shard_map/ppermute | solution.py:26
  18.1 0.0 collective-permute-start.9
  18.1 1.2 %first.2 = bf16[192,8,128]{2,1,0:T(8,128)(2,1)S(1)} custom-call(s32[1]{0:T(128)} %bitcast.side_ref, s32[1]{0:T(128)} %bitcast.1.place_ref, bf16[192,32,128]{2,1,0:T(8,128)(2,1)} %src.2), custom_call_target="tpu_custom_call" | custom-call | tf_op jit(solution)/shard_map/first/pallas_call | solution.py:76
  19.3 0.0 copy-start
  19.3 1.8 %collective-permute-start.10 = (bf16[192,8,128]{2,1,0:T(8,128)(2,1)S(1)}, bf16[192,8,128]{2,1,0:T(8,128)(2,1)S(1)}, u32[]{:S(2)}, u32[]{:S(2)}) collective-permute-start(bf16[192,8,128]{2,1,0:T(8,128)(2,1)S(1)} %first.2), channel_id=1, source_target_pairs={{0,1},{1,0},{2,3},{3,2},{4,5},{5,4},{6,7},{7,6},{8,9},{9,8},{10,11... | collective-permute-start | bytes 1179656 | tf_op jit(solution)/shard_map/ppermute | solution.py:30
  21.1 1.1 %first.3 = bf16[192,8,128]{2,1,0:T(8,128)(2,1)S(1)} custom-call(s32[1]{0:T(128)} %bitcast.side_ref, s32[1]{0:T(128)} %bitcast.1.place_ref, bf16[192,32,128]{2,1,0:T(8,128)(2,1)} %src.3), custom_call_target="tpu_custom_call" | custom-call | tf_op jit(solution)/shard_map/first/pallas_call | solution.py:76
  22.2 0.0 copy-start.2
  22.2 0.0 copy-start.3
  22.2 0.5 collective-permute-start.11
  22.7 0.7 rest.1
  23.4 0.2 copy-done.2
  23.6 1.7 %row_stats.1 = (f32[2,4,768]{2,1,0:T(4,128)S(1)}, f32[2,4,768]{2,1,0:T(4,128)S(1)}) custom-call(s32[1]{0:T(128)} %bitcast.side_ref, bf16[192,32,128]{2,1,0:T(8,128)(2,1)S(1)} %copy-done, bf16[192,32,128]{2,1,0:T(8,128)(2,1)S(1)} %copy-done.2, f32[32,192]{1,0:T(8,128)S(1)} %bitcast.7), custom_call_target="tpu_custom_call" | custom-call | tf_op jit(solution)/shard_map/row_stats/pallas_call | solution.py:214
  25.3 1.0 %collective-permute-done.2.far = bf16[2,2,384,128]{3,2,1,0:T(8,128)(2,1)S(1)} collective-permute-done((bf16[2,2,384,128]{3,2,1,0:T(8,128)(2,1)S(1)}, bf16[2,2,384,128]{3,2,1,0:T(8,128)(2,1)S(1)}, u32[]{:S(2)}, u32[]{:S(2)}) %collective-permute-start.2) | collective-permute-done | bytes 393248 | tf_op jit(solution)/shard_map/ppermute | solution.py:26
  26.3 1.5 %collective-permute-start.1 = (f32[2,4,768]{2,1,0:T(4,128)S(1)}, f32[2,4,768]{2,1,0:T(4,128)S(1)}, u32[]{:S(2)}, u32[]{:S(2)}) collective-permute-start(f32[2,4,768]{2,1,0:T(4,128)S(1)} %get-tuple-element.35), channel_id=1, source_target_pairs={{0,1},{1,0},{2,3},{3,2},{4,5},{5,4},{6,7},{7,6},{8,9},{9,8},{10,11... | collective-permute-start | bytes 73736 | tf_op jit(solution)/shard_map/ppermute | solution.py:30
  27.8 0.5 collective-permute-start
  28.3 3.9 %attention.8 = (bf16[2,768,128]{2,1,0:T(8,128)(2,1)S(1)}, f32[2,1152,128]{2,1,0:T(8,128)S(1)}, f32[2,1152,128]{2,1,0:T(8,128)S(1)}) custom-call(s32[1]{0:T(128)} %bitcast.side_ref, s32[1]{0:T(128)} %bitcast.1.place_ref, bf16[2,768,128]{2,1,0:T(8,128)(2,1)S(1)} %get-tuple-element.46.q, bf16[2,768,128]{2,1,0:T(8,128)(2,1)S(1)} %get-tuple-element.47.g, ...), custom_call_target="tpu_custom_call" | custom-call | flops 1635778560 | tf_op jit(solution)/shard_map/attention/pallas_call | solution.py:425
  32.2 8.1 %collective-permute-done.1.stats = f32[2,4,768]{2,1,0:T(4,128)S(1)} collective-permute-done((f32[2,4,768]{2,1,0:T(4,128)S(1)}, f32[2,4,768]{2,1,0:T(4,128)S(1)}, u32[]{:S(2)}, u32[]{:S(2)}) %collective-permute-start.1) | collective-permute-done | bytes 24608 | tf_op jit(solution)/shard_map/ppermute | solution.py:30
  40.3 1.7 %collective-permute-start.6 = (bf16[2,768,128]{2,1,0:T(8,128)(2,1)S(1)}, bf16[2,768,128]{2,1,0:T(8,128)(2,1)S(1)}, u32[]{:S(2)}, u32[]{:S(2)}) collective-permute-start(bf16[2,768,128]{2,1,0:T(8,128)(2,1)S(1)} %get-tuple-element.43), channel_id=1, source_target_pairs={{0,1},{1,0},{2,3},{3,2},{4,5},{5,4},{6,7},{7,6},{8,9},{9,8},{10,11... | collective-permute-start | bytes 1179656 | tf_op jit(solution)/shard_map/ppermute | solution.py:30
  42.0 3.9 %attention.9 = (bf16[2,768,128]{2,1,0:T(8,128)(2,1)S(1)}, f32[2,1152,128]{2,1,0:T(8,128)S(1)}, f32[2,1152,128]{2,1,0:T(8,128)S(1)}, bf16[2,2,384,128]{3,2,1,0:T(8,128)(2,1)S(1)}) custom-call(s32[1]{0:T(128)} %bitcast.side_ref, s32[1]{0:T(128)} %bitcast.1.place_ref, ...), custom_call_target="tpu_custom_call", output_to_operand_aliasing={{1}: (9, {}), {2}: (10, {})} | custom-call | flops 1635778560 | tf_op jit(solution)/shard_map/attention/pallas_call | solution.py:425
  46.0 0.1 collective-permute-start.15
  46.1 0.4 collective-permute-start.12
  46.4 4.1 %attention.5 = (bf16[2,768,128]{2,1,0:T(8,128)(2,1)S(1)}, f32[2,1152,128]{2,1,0:T(8,128)S(1)}, f32[2,1152,128]{2,1,0:T(8,128)S(1)}) custom-call(s32[1]{0:T(128)} %bitcast.side_ref, s32[1]{0:T(128)} %bitcast.1.place_ref, bf16[2,768,128]{2,1,0:T(8,128)(2,1)S(1)} %get-tuple-element.38.q, bf16[2,768,128]{2,1,0:T(8,128)(2,1)S(1)} %get-tuple-element.39.g, ...), custom_call_target="tpu_custom_call" | custom-call | flops 1635778560 | tf_op jit(solution)/shard_map/attention/pallas_call | solution.py:425
  50.5 2.0 %attention.6 = (bf16[1,768,128]{2,1,0:T(8,128)(2,1)S(1)}, f32[2,1152,128]{2,1,0:T(8,128)S(1)}, bf16[2,1,384,128]{3,2,1,0:T(8,128)(2,1)S(1)}) custom-call(s32[1]{0:T(128)} %bitcast.side_ref, s32[1]{0:T(128)} %bitcast.1.place_ref, bf16[2,768,128]{2,1,0:T(8,128)(2,1)S(1)} %collective-permute-done.q.g, ...), custom_call_target="tpu_custom_call", output_to_operand_aliasing={{1}: (9, {})} | custom-call | flops 817889280 | tf_op jit(solution)/shard_map/attention/pallas_call | solution.py:425
  52.5 0.2 collective-permute-start.16
  52.7 4.5 %collective-permute-done.6.q.g = bf16[2,768,128]{2,1,0:T(8,128)(2,1)S(1)} collective-permute-done((bf16[2,768,128]{2,1,0:T(8,128)(2,1)S(1)}, bf16[2,768,128]{2,1,0:T(8,128)(2,1)S(1)}, u32[]{:S(2)}, u32[]{:S(2)}) %collective-permute-start.6) | collective-permute-done | bytes 393248 | tf_op jit(solution)/shard_map/ppermute | solution.py:30
  57.2 1.9 %attention.7 = (bf16[1,768,128]{2,1,0:T(8,128)(2,1)S(1)}, f32[2,1152,128]{2,1,0:T(8,128)S(1)}, bf16[2,1,384,128]{3,2,1,0:T(8,128)(2,1)S(1)}) custom-call(s32[1]{0:T(128)} %bitcast.side_ref, s32[1]{0:T(128)} %bitcast.1.place_ref, bf16[2,768,128]{2,1,0:T(8,128)(2,1)S(1)} %collective-permute-done.6.q.g, ...), custom_call_target="tpu_custom_call", output_to_operand_aliasing={{1}: (9, {})} | custom-call | flops 817889280 | tf_op jit(solution)/shard_map/attention/pallas_call | solution.py:425
  59.1 0.1 collective-permute-start.13
  59.2 0.1 merge.4
  59.3 2.0 %collective-permute-start.17 = (bf16[2,2,384,128]{3,2,1,0:T(8,128)(2,1)S(1)}, bf16[2,2,384,128]{3,2,1,0:T(8,128)(2,1)S(1)}, u32[]{:S(2)}, u32[]{:S(2)}) collective-permute-start(bf16[2,2,384,128]{3,2,1,0:T(8,128)(2,1)S(1)} %merge.4), channel_id=1, source_target_pairs={{0,28},{2,30},{4,0},{6,2},{8,4},{10,6},{12,8},{14,10},{16,12},{18,... | collective-permute-start | bytes 1179656 | tf_op jit(solution)/shard_map/ppermute | solution.py:26
  61.4 1.5 %collective-permute-start.7 = (bf16[1,768,128]{2,1,0:T(8,128)(2,1)S(1)}, bf16[1,768,128]{2,1,0:T(8,128)(2,1)S(1)}, u32[]{:S(2)}, u32[]{:S(2)}) collective-permute-start(bf16[1,768,128]{2,1,0:T(8,128)(2,1)S(1)} %get-tuple-element.45), channel_id=1, source_target_pairs={{0,1},{1,0},{2,3},{3,2},{4,5},{5,4},{6,7},{7,6},{8,9},{9,8},{10,11... | collective-permute-start | bytes 589832 | tf_op jit(solution)/shard_map/ppermute | solution.py:30
  62.9 0.5 collective-permute-start.5
  63.4 0.1 merge.5
  63.5 1.5 %collective-permute-start.18 = (bf16[2,1,384,128]{3,2,1,0:T(8,128)(2,1)S(1)}, bf16[2,1,384,128]{3,2,1,0:T(8,128)(2,1)S(1)}, u32[]{:S(2)}, u32[]{:S(2)}) collective-permute-start(bf16[2,1,384,128]{3,2,1,0:T(8,128)(2,1)S(1)} %merge.5), channel_id=1, source_target_pairs={{0,28},{2,30},{4,0},{6,2},{8,4},{10,6},{12,8},{14,10},{16,12},{18,... | collective-permute-start | bytes 589832 | tf_op jit(solution)/shard_map/ppermute | solution.py:26
  65.0 0.1 merge.3
  65.0 0.6 collective-permute-done.12.refs_2_
  65.6 2.0 %collective-permute-start.14 = (bf16[2,1,384,128]{3,2,1,0:T(8,128)(2,1)S(1)}, bf16[2,1,384,128]{3,2,1,0:T(8,128)(2,1)S(1)}, u32[]{:S(2)}, u32[]{:S(2)}) collective-permute-start(bf16[2,1,384,128]{3,2,1,0:T(8,128)(2,1)S(1)} %merge.3), channel_id=1, source_target_pairs={{0,28},{2,30},{4,0},{6,2},{8,4},{10,6},{12,8},{14,10},{16,12},{18,... | collective-permute-start | bytes 589832 | tf_op jit(solution)/shard_map/ppermute | solution.py:26
  67.6 1.1 %place.2.refs_2_ = bf16[192,32,128]{2,1,0:T(8,128)(2,1)} custom-call(s32[1]{0:T(128)} %bitcast.side_ref, bf16[2,768,128]{2,1,0:T(8,128)(2,1)S(1)} %get-tuple-element.49.refs_0_, bf16[2,768,128]{2,1,0:T(8,128)(2,1)S(1)} %get-tuple-element.50.refs_1_, bf16[2,768,128]{2,1,0:T(8,128)(2,1)S(1)} %collective-permute-done.12.refs_2_), custom_call_target="tpu_custom_call" | custom-call | tf_op jit(solution)/shard_map/place/pallas_call | solution.py:317
  68.8 1.1 %collective-permute-done.7.refs_1_ = bf16[1,768,128]{2,1,0:T(8,128)(2,1)S(1)} collective-permute-done((bf16[1,768,128]{2,1,0:T(8,128)(2,1)S(1)}, bf16[1,768,128]{2,1,0:T(8,128)(2,1)S(1)}, u32[]{:S(2)}, u32[]{:S(2)}) %collective-permute-start.7) | collective-permute-done | bytes 196640 | tf_op jit(solution)/shard_map/ppermute | solution.py:30
  69.8 3.8 %collective-permute-done.5.refs_0_ = bf16[1,768,128]{2,1,0:T(8,128)(2,1)S(1)} collective-permute-done((bf16[1,768,128]{2,1,0:T(8,128)(2,1)S(1)}, bf16[1,768,128]{2,1,0:T(8,128)(2,1)S(1)}, u32[]{:S(2)}, u32[]{:S(2)}) %collective-permute-start.5) | collective-permute-done | bytes 196640 | tf_op jit(solution)/shard_map/ppermute | solution.py:30
  73.6 0.8 %place.3 = bf16[192,32,128]{2,1,0:T(8,128)(2,1)} custom-call(s32[1]{0:T(128)} %bitcast.side_ref, bf16[1,768,128]{2,1,0:T(8,128)(2,1)S(1)} %collective-permute-done.5.refs_0_, bf16[1,768,128]{2,1,0:T(8,128)(2,1)S(1)} %collective-permute-done.7.refs_1_, bf16[192,32,128]{2,1,0:T(8,128)(2,1)} %place.2.refs_2_), custom_call_target="tpu_custom_call", output_to_operand_aliasing={{}: (3, {})} | custom-call | tf_op jit(solution)/shard_map/place/pallas_call | solution.py:317
  74.4 1.1 %collective-permute-done.18.refs_8_ = bf16[2,1,384,128]{3,2,1,0:T(8,128)(2,1)S(1)} collective-permute-done((bf16[2,1,384,128]{3,2,1,0:T(8,128)(2,1)S(1)}, bf16[2,1,384,128]{3,2,1,0:T(8,128)(2,1)S(1)}, u32[]{:S(2)}, u32[]{:S(2)}) %collective-permute-start.18) | collective-permute-done | bytes 196640 | tf_op jit(solution)/shard_map/ppermute | solution.py:26
  75.6 0.3 gather.1
  75.9 3.4 %collective-permute-done.14.last = bf16[2,1,384,128]{3,2,1,0:T(8,128)(2,1)S(1)} collective-permute-done((bf16[2,1,384,128]{3,2,1,0:T(8,128)(2,1)S(1)}, bf16[2,1,384,128]{3,2,1,0:T(8,128)(2,1)S(1)}, u32[]{:S(2)}, u32[]{:S(2)}) %collective-permute-start.14) | collective-permute-done | bytes 196640 | tf_op jit(solution)/shard_map/ppermute | solution.py:26
  79.3 1.0 %join.1 = (bf16[1536,128]{1,0:T(8,128)(2,1)}, bf16[1536,128]{1,0:T(8,128)(2,1)}, f32[1536,128]{1,0:T(8,128)S(1)}, f32[1536,128]{1,0:T(8,128)S(1)}) custom-call(s32[1]{0:T(128)} %bitcast.1.place_ref, bf16[2,1,384,128]{3,2,1,0:T(8,128)(2,1)S(1)} %collective-permute-done.14.last, ...), custom_call_target="tpu_custom_call", output_to_operand_aliasing={{2}: (2, {}), {3}: (3, {})} | custom-call | tf_op jit(solution)/shard_map/join/pallas_call | solution.py:268
  (15 shorter events, 0.0 us)
Async XLA Ops:
  2.0 25.8 %collective-permute-start.4 = (bf16[2,4,384,128]{3,2,1,0:T(8,128)(2,1)S(1)}, bf16[2,4,384,128]{3,2,1,0:T(8,128)(2,1)S(1)}, u32[]{:S(2)}, u32[]{:S(2)}) collective-permute-start(bf16[2,4,384,128]{3,2,1,0:T(8,128)(2,1)S(1)} %get-tuple-element.37.own), channel_id=1, source_target_pairs={{0,2},{2,0},{4,6},{6,4},{8,10},{10,8},{12,14},{14,12},{16,18},{18,... | collective-permute-start | bytes 2359304 | tf_op jit(solution)/shard_map/ppermute | solution.py:30
  2.6 15.5 %collective-permute-start.8 = (bf16[2,2,384,128]{3,2,1,0:T(8,128)(2,1)S(1)}, bf16[2,2,384,128]{3,2,1,0:T(8,128)(2,1)S(1)}, u32[]{:S(2)}, u32[]{:S(2)}) collective-permute-start(bf16[2,2,384,128]{3,2,1,0:T(8,128)(2,1)S(1)} %get-tuple-element.48), channel_id=1, source_target_pairs={{0,4},{2,6},{4,8},{6,10},{8,12},{10,14},{12,16},{14,18},{16,20},{1... | collective-permute-start | bytes 1179656 | tf_op jit(solution)/shard_map/ppermute | solution.py:26
  5.1 21.2 %collective-permute-start.2 = (bf16[2,2,384,128]{3,2,1,0:T(8,128)(2,1)S(1)}, bf16[2,2,384,128]{3,2,1,0:T(8,128)(2,1)S(1)}, u32[]{:S(2)}, u32[]{:S(2)}) collective-permute-start(bf16[2,2,384,128]{3,2,1,0:T(8,128)(2,1)S(1)} %get-tuple-element.36), channel_id=1, source_target_pairs={{0,4},{2,6},{4,8},{6,10},{8,12},{10,14},{12,16},{14,18},{16,20},{1... | collective-permute-start | bytes 1179656 | tf_op jit(solution)/shard_map/ppermute | solution.py:26
  18.1 10.2 %collective-permute-start.9 = (bf16[2,2,384,128]{3,2,1,0:T(8,128)(2,1)S(1)}, bf16[2,2,384,128]{3,2,1,0:T(8,128)(2,1)S(1)}, u32[]{:S(2)}, u32[]{:S(2)}) collective-permute-start(bf16[2,2,384,128]{3,2,1,0:T(8,128)(2,1)S(1)} %collective-permute-done.8.far), channel_id=1, source_target_pairs={{0,2},{2,0},{4,6},{6,4},{8,10},{10,8},{12,14},{14,12},{16,18},{18,... | collective-permute-start | bytes 1179656 | tf_op jit(solution)/shard_map/ppermute | solution.py:30
  18.1 4.6 %copy-start.1 = (bf16[192,32,128]{2,1,0:T(8,128)(2,1)S(1)}, bf16[192,32,128]{2,1,0:T(8,128)(2,1)}, u32[]{:S(2)}) copy-start(bf16[192,32,128]{2,1,0:T(8,128)(2,1)} %src.2) | copy-start | bytes 4718596
  19.3 3.4 %copy-start = (bf16[192,32,128]{2,1,0:T(8,128)(2,1)S(1)}, bf16[192,32,128]{2,1,0:T(8,128)(2,1)}, u32[]{:S(2)}) copy-start(bf16[192,32,128]{2,1,0:T(8,128)(2,1)} %src.3) | copy-start | bytes 4718596
  19.3 22.7 %collective-permute-start.10 = (bf16[192,8,128]{2,1,0:T(8,128)(2,1)S(1)}, bf16[192,8,128]{2,1,0:T(8,128)(2,1)S(1)}, u32[]{:S(2)}, u32[]{:S(2)}) collective-permute-start(bf16[192,8,128]{2,1,0:T(8,128)(2,1)S(1)} %first.2), channel_id=1, source_target_pairs={{0,1},{1,0},{2,3},{3,2},{4,5},{5,4},{6,7},{7,6},{8,9},{9,8},{10,11... | collective-permute-start | bytes 1179656 | tf_op jit(solution)/shard_map/ppermute | solution.py:30
  22.2 1.4 %copy-start.2 = (bf16[192,32,128]{2,1,0:T(8,128)(2,1)S(1)}, bf16[192,32,128]{2,1,0:T(8,128)(2,1)}, u32[]{:S(2)}) copy-start(bf16[192,32,128]{2,1,0:T(8,128)(2,1)} %o.1) | copy-start | bytes 4718596
  22.2 1.4 %copy-start.3 = (f32[192,32]{0,1:T(8,128)S(1)}, f32[192,32]{0,1:T(8,128)}, u32[]{:S(2)}) copy-start(f32[192,32]{0,1:T(8,128)} %param.11) | copy-start | bytes 73732
  22.2 19.8 %collective-permute-start.11 = (bf16[192,8,128]{2,1,0:T(8,128)(2,1)S(1)}, bf16[192,8,128]{2,1,0:T(8,128)(2,1)S(1)}, u32[]{:S(2)}, u32[]{:S(2)}) collective-permute-start(bf16[192,8,128]{2,1,0:T(8,128)(2,1)S(1)} %first.3), channel_id=1, source_target_pairs={{0,1},{1,0},{2,3},{3,2},{4,5},{5,4},{6,7},{7,6},{8,9},{9,8},{10,11... | collective-permute-start | bytes 1179656 | tf_op jit(solution)/shard_map/ppermute | solution.py:30
  26.3 14.0 %collective-permute-start.1 = (f32[2,4,768]{2,1,0:T(4,128)S(1)}, f32[2,4,768]{2,1,0:T(4,128)S(1)}, u32[]{:S(2)}, u32[]{:S(2)}) collective-permute-start(f32[2,4,768]{2,1,0:T(4,128)S(1)} %get-tuple-element.35), channel_id=1, source_target_pairs={{0,1},{1,0},{2,3},{3,2},{4,5},{5,4},{6,7},{7,6},{8,9},{9,8},{10,11... | collective-permute-start | bytes 73736 | tf_op jit(solution)/shard_map/ppermute | solution.py:30
  27.8 22.7 %collective-permute-start = (bf16[2,768,128]{2,1,0:T(8,128)(2,1)S(1)}, bf16[2,768,128]{2,1,0:T(8,128)(2,1)S(1)}, u32[]{:S(2)}, u32[]{:S(2)}) collective-permute-start(bf16[2,768,128]{2,1,0:T(8,128)(2,1)S(1)} %get-tuple-element.34), channel_id=1, source_target_pairs={{0,1},{1,0},{2,3},{3,2},{4,5},{5,4},{6,7},{7,6},{8,9},{9,8},{10,11... | collective-permute-start | bytes 1179656 | tf_op jit(solution)/shard_map/ppermute | solution.py:30
  28.3 18.1 %collective-permute-start.3 = (bf16[2,2,384,128]{3,2,1,0:T(8,128)(2,1)S(1)}, bf16[2,2,384,128]{3,2,1,0:T(8,128)(2,1)S(1)}, u32[]{:S(2)}, u32[]{:S(2)}) collective-permute-start(bf16[2,2,384,128]{3,2,1,0:T(8,128)(2,1)S(1)} %collective-permute-done.2.far), channel_id=1, source_target_pairs={{0,2},{2,0},{4,6},{6,4},{8,10},{10,8},{12,14},{14,12},{16,18},{18,... | collective-permute-start | bytes 1179656 | tf_op jit(solution)/shard_map/ppermute | solution.py:30
  40.3 16.9 %collective-permute-start.6 = (bf16[2,768,128]{2,1,0:T(8,128)(2,1)S(1)}, bf16[2,768,128]{2,1,0:T(8,128)(2,1)S(1)}, u32[]{:S(2)}, u32[]{:S(2)}) collective-permute-start(bf16[2,768,128]{2,1,0:T(8,128)(2,1)S(1)} %get-tuple-element.43), channel_id=1, source_target_pairs={{0,1},{1,0},{2,3},{3,2},{4,5},{5,4},{6,7},{7,6},{8,9},{9,8},{10,11... | collective-permute-start | bytes 1179656 | tf_op jit(solution)/shard_map/ppermute | solution.py:30
  46.0 13.2 %collective-permute-start.15 = (bf16[2,2,384,128]{3,2,1,0:T(8,128)(2,1)S(1)}, bf16[2,2,384,128]{3,2,1,0:T(8,128)(2,1)S(1)}, u32[]{:S(2)}, u32[]{:S(2)}) collective-permute-start(bf16[2,2,384,128]{3,2,1,0:T(8,128)(2,1)S(1)} %get-tuple-element.59), channel_id=1, source_target_pairs={{0,2},{2,0},{4,6},{6,4},{8,10},{10,8},{12,14},{14,12},{16,18},{18,... | collective-permute-start | bytes 1179656 | tf_op jit(solution)/shard_map/ppermute | solution.py:30
  46.1 19.5 %collective-permute-start.12 = (bf16[2,768,128]{2,1,0:T(8,128)(2,1)S(1)}, bf16[2,768,128]{2,1,0:T(8,128)(2,1)S(1)}, u32[]{:S(2)}, u32[]{:S(2)}) collective-permute-start(bf16[2,768,128]{2,1,0:T(8,128)(2,1)S(1)} %get-tuple-element.53), channel_id=1, source_target_pairs={{0,1},{1,0},{2,3},{3,2},{4,5},{5,4},{6,7},{7,6},{8,9},{9,8},{10,11... | collective-permute-start | bytes 1179656 | tf_op jit(solution)/shard_map/ppermute | solution.py:30
  52.5 10.4 %collective-permute-start.16 = (bf16[2,1,384,128]{3,2,1,0:T(8,128)(2,1)S(1)}, bf16[2,1,384,128]{3,2,1,0:T(8,128)(2,1)S(1)}, u32[]{:S(2)}, u32[]{:S(2)}) collective-permute-start(bf16[2,1,384,128]{3,2,1,0:T(8,128)(2,1)S(1)} %get-tuple-element.60), channel_id=1, source_target_pairs={{0,2},{2,0},{4,6},{6,4},{8,10},{10,8},{12,14},{14,12},{16,18},{18,... | collective-permute-start | bytes 589832 | tf_op jit(solution)/shard_map/ppermute | solution.py:30
  59.1 4.3 %collective-permute-start.13 = (bf16[2,1,384,128]{3,2,1,0:T(8,128)(2,1)S(1)}, bf16[2,1,384,128]{3,2,1,0:T(8,128)(2,1)S(1)}, u32[]{:S(2)}, u32[]{:S(2)}) collective-permute-start(bf16[2,1,384,128]{3,2,1,0:T(8,128)(2,1)S(1)} %get-tuple-element.55), channel_id=1, source_target_pairs={{0,2},{2,0},{4,6},{6,4},{8,10},{10,8},{12,14},{14,12},{16,18},{18,... | collective-permute-start | bytes 589832 | tf_op jit(solution)/shard_map/ppermute | solution.py:30
  59.3 16.3 %collective-permute-start.17 = (bf16[2,2,384,128]{3,2,1,0:T(8,128)(2,1)S(1)}, bf16[2,2,384,128]{3,2,1,0:T(8,128)(2,1)S(1)}, u32[]{:S(2)}, u32[]{:S(2)}) collective-permute-start(bf16[2,2,384,128]{3,2,1,0:T(8,128)(2,1)S(1)} %merge.4), channel_id=1, source_target_pairs={{0,28},{2,30},{4,0},{6,2},{8,4},{10,6},{12,8},{14,10},{16,12},{18,... | collective-permute-start | bytes 1179656 | tf_op jit(solution)/shard_map/ppermute | solution.py:26
  61.4 8.4 %collective-permute-start.7 = (bf16[1,768,128]{2,1,0:T(8,128)(2,1)S(1)}, bf16[1,768,128]{2,1,0:T(8,128)(2,1)S(1)}, u32[]{:S(2)}, u32[]{:S(2)}) collective-permute-start(bf16[1,768,128]{2,1,0:T(8,128)(2,1)S(1)} %get-tuple-element.45), channel_id=1, source_target_pairs={{0,1},{1,0},{2,3},{3,2},{4,5},{5,4},{6,7},{7,6},{8,9},{9,8},{10,11... | collective-permute-start | bytes 589832 | tf_op jit(solution)/shard_map/ppermute | solution.py:30
  62.9 10.7 %collective-permute-start.5 = (bf16[1,768,128]{2,1,0:T(8,128)(2,1)S(1)}, bf16[1,768,128]{2,1,0:T(8,128)(2,1)S(1)}, u32[]{:S(2)}, u32[]{:S(2)}) collective-permute-start(bf16[1,768,128]{2,1,0:T(8,128)(2,1)S(1)} %get-tuple-element.42), channel_id=1, source_target_pairs={{0,1},{1,0},{2,3},{3,2},{4,5},{5,4},{6,7},{7,6},{8,9},{9,8},{10,11... | collective-permute-start | bytes 589832 | tf_op jit(solution)/shard_map/ppermute | solution.py:30
  63.5 12.1 %collective-permute-start.18 = (bf16[2,1,384,128]{3,2,1,0:T(8,128)(2,1)S(1)}, bf16[2,1,384,128]{3,2,1,0:T(8,128)(2,1)S(1)}, u32[]{:S(2)}, u32[]{:S(2)}) collective-permute-start(bf16[2,1,384,128]{3,2,1,0:T(8,128)(2,1)S(1)} %merge.5), channel_id=1, source_target_pairs={{0,28},{2,30},{4,0},{6,2},{8,4},{10,6},{12,8},{14,10},{16,12},{18,... | collective-permute-start | bytes 589832 | tf_op jit(solution)/shard_map/ppermute | solution.py:26
  65.6 13.7 %collective-permute-start.14 = (bf16[2,1,384,128]{3,2,1,0:T(8,128)(2,1)S(1)}, bf16[2,1,384,128]{3,2,1,0:T(8,128)(2,1)S(1)}, u32[]{:S(2)}, u32[]{:S(2)}) collective-permute-start(bf16[2,1,384,128]{3,2,1,0:T(8,128)(2,1)S(1)} %merge.3), channel_id=1, source_target_pairs={{0,28},{2,30},{4,0},{6,2},{8,4},{10,6},{12,8},{14,10},{16,12},{18,... | collective-permute-start | bytes 589832 | tf_op jit(solution)/shard_map/ppermute | solution.py:26

commit v2 on v1

--- a/solution.py
+++ b/solution.py
@@ -305,9 +305,15 @@
     for m, (a, b, ours, first) in enumerate(plan):
         side = side_ref[0] if ours else 1 - side_ref[0]
         start = pl.multiple_of(side * heads + first, pair)
-        buf[m] = tangle(refs[a[0]][a[1]], refs[b[0]][b[1]], tokens)
-        copies.append(pltpu.make_async_copy(buf.at[m], out.at[:, pl.ds(start, pair), :], sem.at[m]))
-        copies[-1].start()
+        rows = refs[a[0]].shape[1]
+        parts = sem.shape[1]
+        for j in range(parts):
+            some = pl.ds(j * (rows // parts), rows // parts)
+            here = pl.ds(j * (tokens // parts), tokens // parts)
+            buf[m, here] = tangle(refs[a[0]][a[1], some, :], refs[b[0]][b[1], some, :], tokens // parts)
+            view = out.at[here, pl.ds(start, pair), :]
+            copies.append(pltpu.make_async_copy(buf.at[m, here], view, sem.at[m, j]))
+            copies[-1].start()
     for copy in copies:
         copy.wait()
 
@@ -321,7 +327,7 @@
         out_shape=jax.ShapeDtypeStruct(shape, BF16),
         scratch_shapes=[
             pltpu.VMEM((len(plan), shape[0], pair, shape[2]), BF16),
-            pltpu.SemaphoreType.DMA((len(plan),)),
+            pltpu.SemaphoreType.DMA((len(plan), 4)),
         ],
         input_output_aliases={1 + len(pieces): 0} if more else {},
         compiler_params=params(4),

time: 80.6 us -> 80.6 us (level)
  transfers between devices with their start and end apart: 19 -> 19, of which waited for: 9 -> 9; matrix products, arithmetic and copies ran while one was open for 0% -> 0% of each run, Pallas kernels for 29% -> 28%
where the time goes in v2:
time: 80.6 us; the launch traced here: 80.3 us
  waiting for transfers between devices  35.2 us (44%)
  Pallas kernels  25.3 us (31%)
  starting transfers between devices  18.9 us (23%)
  between operations  0.82 us (1%)
    ppermute x14, waiting for transfers between devices, swapped(): lax.ppermute(shard, axis, [(i, i ^ 1) for i in range(lax.axis_size(axis))])  18.1 us
    ppermute x5, waiting for transfers between devices, turned(): lax.ppermute(shard, axis, [(i, (i + by) % size) for i in range(size)])  17.1 us
    pallas_call x5, Pallas kernels, attention(): pl.pallas_call(functools.partial(attn_kernel, scale, spots, ours, add), i...  15.8 us
    ppermute x5, starting transfers between devices, turned(): lax.ppermute(shard, axis, [(i, (i + by) % size) for i in range(size)])  9.64 us
    ppermute x14, starting transfers between devices, swapped(): lax.ppermute(shard, axis, [(i, i ^ 1) for i in range(lax.axis_size(axis))])  9.25 us
    pallas_call x2, Pallas kernels, first(): pl.pallas_call(functools.partial(first_kernel, heads, pair), in_specs=[SM...  2.27 us
    pallas_call x2, Pallas kernels, place(): pl.pallas_call(functools.partial(place_kernel, plan, heads), in_specs=[SM...  1.92 us
    pallas_call x1, Pallas kernels, row_stats(): pl.pallas_call(functools.partial(stats_kernel, per), in_specs=[SMEM, VMEM...  1.66 us
  transfers between devices with their start and end apart: 19, of which 9 were waited for; matrix products, arithmetic and copies ran while one was open for 0% of the time, Pallas kernels for 28%

profile of v2, /device:TPU:0, one launch (start us, length us, event | category | flops | bytes accessed | tf_op | source)
XLA Modules:
  0.0 80.3 jit_solution(7604147138637795401)
XLA Ops:
  0.6 1.4 %split.1 = (bf16[2,4,384,128]{3,2,1,0:T(8,128)(2,1)S(1)}, bf16[2,2,384,128]{3,2,1,0:T(8,128)(2,1)S(1)}, bf16[2,2,384,128]{3,2,1,0:T(8,128)(2,1)S(1)}) custom-call(bf16[1536,128]{1,0:T(8,128)(2,1)} %bitcast.8, bf16[1536,128]{1,0:T(8,128)(2,1)} %bitcast.9), custom_call_target="tpu_custom_call" | custom-call | tf_op jit(solution)/shard_map/split/pallas_call | solution.py:143
  2.0 0.6 collective-permute-start.4
  2.6 2.5 %collective-permute-start.8 = (bf16[2,2,384,128]{3,2,1,0:T(8,128)(2,1)S(1)}, bf16[2,2,384,128]{3,2,1,0:T(8,128)(2,1)S(1)}, u32[]{:S(2)}, u32[]{:S(2)}) collective-permute-start(bf16[2,2,384,128]{3,2,1,0:T(8,128)(2,1)S(1)} %get-tuple-element.48), channel_id=1, source_target_pairs={{0,4},{2,6},{4,8},{6,10},{8,12},{10,14},{12,16},{14,18},{16,20},{1... | collective-permute-start | bytes 1179656 | tf_op jit(solution)/shard_map/ppermute | solution.py:26
  5.1 1.5 %collective-permute-start.2 = (bf16[2,2,384,128]{3,2,1,0:T(8,128)(2,1)S(1)}, bf16[2,2,384,128]{3,2,1,0:T(8,128)(2,1)S(1)}, u32[]{:S(2)}, u32[]{:S(2)}) collective-permute-start(bf16[2,2,384,128]{3,2,1,0:T(8,128)(2,1)S(1)} %get-tuple-element.36), channel_id=1, source_target_pairs={{0,4},{2,6},{4,8},{6,10},{8,12},{10,14},{12,16},{14,18},{16,20},{1... | collective-permute-start | bytes 1179656 | tf_op jit(solution)/shard_map/ppermute | solution.py:26
  6.6 11.5 %collective-permute-done.8.far = bf16[2,2,384,128]{3,2,1,0:T(8,128)(2,1)S(1)} collective-permute-done((bf16[2,2,384,128]{3,2,1,0:T(8,128)(2,1)S(1)}, bf16[2,2,384,128]{3,2,1,0:T(8,128)(2,1)S(1)}, u32[]{:S(2)}, u32[]{:S(2)}) %collective-permute-start.8) | collective-permute-done | bytes 393248 | tf_op jit(solution)/shard_map/ppermute | solution.py:26
  18.1 0.0 collective-permute-start.9
  18.1 1.2 %first.2 = bf16[192,8,128]{2,1,0:T(8,128)(2,1)S(1)} custom-call(s32[1]{0:T(128)} %bitcast.side_ref, s32[1]{0:T(128)} %bitcast.1.place_ref, bf16[192,32,128]{2,1,0:T(8,128)(2,1)} %src.2), custom_call_target="tpu_custom_call" | custom-call | tf_op jit(solution)/shard_map/first/pallas_call | solution.py:76
  19.3 0.0 copy-start
  19.3 1.8 %collective-permute-start.10 = (bf16[192,8,128]{2,1,0:T(8,128)(2,1)S(1)}, bf16[192,8,128]{2,1,0:T(8,128)(2,1)S(1)}, u32[]{:S(2)}, u32[]{:S(2)}) collective-permute-start(bf16[192,8,128]{2,1,0:T(8,128)(2,1)S(1)} %first.2), channel_id=1, source_target_pairs={{0,1},{1,0},{2,3},{3,2},{4,5},{5,4},{6,7},{7,6},{8,9},{9,8},{10,11... | collective-permute-start | bytes 1179656 | tf_op jit(solution)/shard_map/ppermute | solution.py:30
  21.1 1.1 %first.3 = bf16[192,8,128]{2,1,0:T(8,128)(2,1)S(1)} custom-call(s32[1]{0:T(128)} %bitcast.side_ref, s32[1]{0:T(128)} %bitcast.1.place_ref, bf16[192,32,128]{2,1,0:T(8,128)(2,1)} %src.3), custom_call_target="tpu_custom_call" | custom-call | tf_op jit(solution)/shard_map/first/pallas_call | solution.py:76
  22.2 0.0 copy-start.2
  22.2 0.0 copy-start.3
  22.2 0.5 collective-permute-start.11
  22.7 0.7 rest.1
  23.4 0.2 copy-done.2
  23.6 1.7 %row_stats.1 = (f32[2,4,768]{2,1,0:T(4,128)S(1)}, f32[2,4,768]{2,1,0:T(4,128)S(1)}) custom-call(s32[1]{0:T(128)} %bitcast.side_ref, bf16[192,32,128]{2,1,0:T(8,128)(2,1)S(1)} %copy-done, bf16[192,32,128]{2,1,0:T(8,128)(2,1)S(1)} %copy-done.2, f32[32,192]{1,0:T(8,128)S(1)} %bitcast.7), custom_call_target="tpu_custom_call" | custom-call | tf_op jit(solution)/shard_map/row_stats/pallas_call | solution.py:214
  25.3 1.0 %collective-permute-done.2.far = bf16[2,2,384,128]{3,2,1,0:T(8,128)(2,1)S(1)} collective-permute-done((bf16[2,2,384,128]{3,2,1,0:T(8,128)(2,1)S(1)}, bf16[2,2,384,128]{3,2,1,0:T(8,128)(2,1)S(1)}, u32[]{:S(2)}, u32[]{:S(2)}) %collective-permute-start.2) | collective-permute-done | bytes 393248 | tf_op jit(solution)/shard_map/ppermute | solution.py:26
  26.3 1.5 %collective-permute-start.1 = (f32[2,4,768]{2,1,0:T(4,128)S(1)}, f32[2,4,768]{2,1,0:T(4,128)S(1)}, u32[]{:S(2)}, u32[]{:S(2)}) collective-permute-start(f32[2,4,768]{2,1,0:T(4,128)S(1)} %get-tuple-element.35), channel_id=1, source_target_pairs={{0,1},{1,0},{2,3},{3,2},{4,5},{5,4},{6,7},{7,6},{8,9},{9,8},{10,11... | collective-permute-start | bytes 73736 | tf_op jit(solution)/shard_map/ppermute | solution.py:30
  27.8 0.5 collective-permute-start
  28.3 3.9 %attention.8 = (bf16[2,768,128]{2,1,0:T(8,128)(2,1)S(1)}, f32[2,1152,128]{2,1,0:T(8,128)S(1)}, f32[2,1152,128]{2,1,0:T(8,128)S(1)}) custom-call(s32[1]{0:T(128)} %bitcast.side_ref, s32[1]{0:T(128)} %bitcast.1.place_ref, bf16[2,768,128]{2,1,0:T(8,128)(2,1)S(1)} %get-tuple-element.46.q, bf16[2,768,128]{2,1,0:T(8,128)(2,1)S(1)} %get-tuple-element.47.g, ...), custom_call_target="tpu_custom_call" | custom-call | flops 1635778560 | tf_op jit(solution)/shard_map/attention/pallas_call | solution.py:431
  32.2 8.1 %collective-permute-done.1.stats = f32[2,4,768]{2,1,0:T(4,128)S(1)} collective-permute-done((f32[2,4,768]{2,1,0:T(4,128)S(1)}, f32[2,4,768]{2,1,0:T(4,128)S(1)}, u32[]{:S(2)}, u32[]{:S(2)}) %collective-permute-start.1) | collective-permute-done | bytes 24608 | tf_op jit(solution)/shard_map/ppermute | solution.py:30
  40.3 1.7 %collective-permute-start.6 = (bf16[2,768,128]{2,1,0:T(8,128)(2,1)S(1)}, bf16[2,768,128]{2,1,0:T(8,128)(2,1)S(1)}, u32[]{:S(2)}, u32[]{:S(2)}) collective-permute-start(bf16[2,768,128]{2,1,0:T(8,128)(2,1)S(1)} %get-tuple-element.43), channel_id=1, source_target_pairs={{0,1},{1,0},{2,3},{3,2},{4,5},{5,4},{6,7},{7,6},{8,9},{9,8},{10,11... | collective-permute-start | bytes 1179656 | tf_op jit(solution)/shard_map/ppermute | solution.py:30
  42.0 3.9 %attention.9 = (bf16[2,768,128]{2,1,0:T(8,128)(2,1)S(1)}, f32[2,1152,128]{2,1,0:T(8,128)S(1)}, f32[2,1152,128]{2,1,0:T(8,128)S(1)}, bf16[2,2,384,128]{3,2,1,0:T(8,128)(2,1)S(1)}) custom-call(s32[1]{0:T(128)} %bitcast.side_ref, s32[1]{0:T(128)} %bitcast.1.place_ref, ...), custom_call_target="tpu_custom_call", output_to_operand_aliasing={{1}: (9, {}), {2}: (10, {})} | custom-call | flops 1635778560 | tf_op jit(solution)/shard_map/attention/pallas_call | solution.py:431
  46.0 0.1 collective-permute-start.15
  46.1 0.4 collective-permute-start.12
  46.4 4.1 %attention.5 = (bf16[2,768,128]{2,1,0:T(8,128)(2,1)S(1)}, f32[2,1152,128]{2,1,0:T(8,128)S(1)}, f32[2,1152,128]{2,1,0:T(8,128)S(1)}) custom-call(s32[1]{0:T(128)} %bitcast.side_ref, s32[1]{0:T(128)} %bitcast.1.place_ref, bf16[2,768,128]{2,1,0:T(8,128)(2,1)S(1)} %get-tuple-element.38.q, bf16[2,768,128]{2,1,0:T(8,128)(2,1)S(1)} %get-tuple-element.39.g, ...), custom_call_target="tpu_custom_call" | custom-call | flops 1635778560 | tf_op jit(solution)/shard_map/attention/pallas_call | solution.py:431
  50.5 2.0 %attention.6 = (bf16[1,768,128]{2,1,0:T(8,128)(2,1)S(1)}, f32[2,1152,128]{2,1,0:T(8,128)S(1)}, bf16[2,1,384,128]{3,2,1,0:T(8,128)(2,1)S(1)}) custom-call(s32[1]{0:T(128)} %bitcast.side_ref, s32[1]{0:T(128)} %bitcast.1.place_ref, bf16[2,768,128]{2,1,0:T(8,128)(2,1)S(1)} %collective-permute-done.q.g, ...), custom_call_target="tpu_custom_call", output_to_operand_aliasing={{1}: (9, {})} | custom-call | flops 817889280 | tf_op jit(solution)/shard_map/attention/pallas_call | solution.py:431
  52.5 0.2 collective-permute-start.16
  52.7 4.5 %collective-permute-done.6.q.g = bf16[2,768,128]{2,1,0:T(8,128)(2,1)S(1)} collective-permute-done((bf16[2,768,128]{2,1,0:T(8,128)(2,1)S(1)}, bf16[2,768,128]{2,1,0:T(8,128)(2,1)S(1)}, u32[]{:S(2)}, u32[]{:S(2)}) %collective-permute-start.6) | collective-permute-done | bytes 393248 | tf_op jit(solution)/shard_map/ppermute | solution.py:30
  57.2 1.9 %attention.7 = (bf16[1,768,128]{2,1,0:T(8,128)(2,1)S(1)}, f32[2,1152,128]{2,1,0:T(8,128)S(1)}, bf16[2,1,384,128]{3,2,1,0:T(8,128)(2,1)S(1)}) custom-call(s32[1]{0:T(128)} %bitcast.side_ref, s32[1]{0:T(128)} %bitcast.1.place_ref, bf16[2,768,128]{2,1,0:T(8,128)(2,1)S(1)} %collective-permute-done.6.q.g, ...), custom_call_target="tpu_custom_call", output_to_operand_aliasing={{1}: (9, {})} | custom-call | flops 817889280 | tf_op jit(solution)/shard_map/attention/pallas_call | solution.py:431
  59.1 0.1 collective-permute-start.13
  59.2 0.1 merge.4
  59.3 2.0 %collective-permute-start.17 = (bf16[2,2,384,128]{3,2,1,0:T(8,128)(2,1)S(1)}, bf16[2,2,384,128]{3,2,1,0:T(8,128)(2,1)S(1)}, u32[]{:S(2)}, u32[]{:S(2)}) collective-permute-start(bf16[2,2,384,128]{3,2,1,0:T(8,128)(2,1)S(1)} %merge.4), channel_id=1, source_target_pairs={{0,28},{2,30},{4,0},{6,2},{8,4},{10,6},{12,8},{14,10},{16,12},{18,... | collective-permute-start | bytes 1179656 | tf_op jit(solution)/shard_map/ppermute | solution.py:26
  61.4 1.5 %collective-permute-start.7 = (bf16[1,768,128]{2,1,0:T(8,128)(2,1)S(1)}, bf16[1,768,128]{2,1,0:T(8,128)(2,1)S(1)}, u32[]{:S(2)}, u32[]{:S(2)}) collective-permute-start(bf16[1,768,128]{2,1,0:T(8,128)(2,1)S(1)} %get-tuple-element.45), channel_id=1, source_target_pairs={{0,1},{1,0},{2,3},{3,2},{4,5},{5,4},{6,7},{7,6},{8,9},{9,8},{10,11... | collective-permute-start | bytes 589832 | tf_op jit(solution)/shard_map/ppermute | solution.py:30
  62.9 0.5 collective-permute-start.5
  63.4 0.1 merge.5
  63.5 1.5 %collective-permute-start.18 = (bf16[2,1,384,128]{3,2,1,0:T(8,128)(2,1)S(1)}, bf16[2,1,384,128]{3,2,1,0:T(8,128)(2,1)S(1)}, u32[]{:S(2)}, u32[]{:S(2)}) collective-permute-start(bf16[2,1,384,128]{3,2,1,0:T(8,128)(2,1)S(1)} %merge.5), channel_id=1, source_target_pairs={{0,28},{2,30},{4,0},{6,2},{8,4},{10,6},{12,8},{14,10},{16,12},{18,... | collective-permute-start | bytes 589832 | tf_op jit(solution)/shard_map/ppermute | solution.py:26
  65.0 0.1 merge.3
  65.0 0.6 collective-permute-done.12.refs_2_
  65.6 2.0 %collective-permute-start.14 = (bf16[2,1,384,128]{3,2,1,0:T(8,128)(2,1)S(1)}, bf16[2,1,384,128]{3,2,1,0:T(8,128)(2,1)S(1)}, u32[]{:S(2)}, u32[]{:S(2)}) collective-permute-start(bf16[2,1,384,128]{3,2,1,0:T(8,128)(2,1)S(1)} %merge.3), channel_id=1, source_target_pairs={{0,28},{2,30},{4,0},{6,2},{8,4},{10,6},{12,8},{14,10},{16,12},{18,... | collective-permute-start | bytes 589832 | tf_op jit(solution)/shard_map/ppermute | solution.py:26
  67.6 1.1 %place.2.refs_2_ = bf16[192,32,128]{2,1,0:T(8,128)(2,1)} custom-call(s32[1]{0:T(128)} %bitcast.side_ref, bf16[2,768,128]{2,1,0:T(8,128)(2,1)S(1)} %get-tuple-element.49.refs_0_, bf16[2,768,128]{2,1,0:T(8,128)(2,1)S(1)} %get-tuple-element.50.refs_1_, bf16[2,768,128]{2,1,0:T(8,128)(2,1)S(1)} %collective-permute-done.12.refs_2_), custom_call_target="tpu_custom_call" | custom-call | tf_op jit(solution)/shard_map/place/pallas_call | solution.py:323
  68.8 1.1 %collective-permute-done.7.refs_1_ = bf16[1,768,128]{2,1,0:T(8,128)(2,1)S(1)} collective-permute-done((bf16[1,768,128]{2,1,0:T(8,128)(2,1)S(1)}, bf16[1,768,128]{2,1,0:T(8,128)(2,1)S(1)}, u32[]{:S(2)}, u32[]{:S(2)}) %collective-permute-start.7) | collective-permute-done | bytes 196640 | tf_op jit(solution)/shard_map/ppermute | solution.py:30
  69.8 3.8 %collective-permute-done.5.refs_0_ = bf16[1,768,128]{2,1,0:T(8,128)(2,1)S(1)} collective-permute-done((bf16[1,768,128]{2,1,0:T(8,128)(2,1)S(1)}, bf16[1,768,128]{2,1,0:T(8,128)(2,1)S(1)}, u32[]{:S(2)}, u32[]{:S(2)}) %collective-permute-start.5) | collective-permute-done | bytes 196640 | tf_op jit(solution)/shard_map/ppermute | solution.py:30
  73.6 0.8 place.3
  74.4 1.2 %collective-permute-done.18.refs_8_ = bf16[2,1,384,128]{3,2,1,0:T(8,128)(2,1)S(1)} collective-permute-done((bf16[2,1,384,128]{3,2,1,0:T(8,128)(2,1)S(1)}, bf16[2,1,384,128]{3,2,1,0:T(8,128)(2,1)S(1)}, u32[]{:S(2)}, u32[]{:S(2)}) %collective-permute-start.18) | collective-permute-done | bytes 196640 | tf_op jit(solution)/shard_map/ppermute | solution.py:26
  75.6 0.3 gather.1
  75.9 3.4 %collective-permute-done.14.last = bf16[2,1,384,128]{3,2,1,0:T(8,128)(2,1)S(1)} collective-permute-done((bf16[2,1,384,128]{3,2,1,0:T(8,128)(2,1)S(1)}, bf16[2,1,384,128]{3,2,1,0:T(8,128)(2,1)S(1)}, u32[]{:S(2)}, u32[]{:S(2)}) %collective-permute-start.14) | collective-permute-done | bytes 196640 | tf_op jit(solution)/shard_map/ppermute | solution.py:26
  79.3 1.0 %join.1 = (bf16[1536,128]{1,0:T(8,128)(2,1)}, bf16[1536,128]{1,0:T(8,128)(2,1)}, f32[1536,128]{1,0:T(8,128)S(1)}, f32[1536,128]{1,0:T(8,128)S(1)}) custom-call(s32[1]{0:T(128)} %bitcast.1.place_ref, bf16[2,1,384,128]{3,2,1,0:T(8,128)(2,1)S(1)} %collective-permute-done.14.last, ...), custom_call_target="tpu_custom_call", output_to_operand_aliasing={{2}: (2, {}), {3}: (3, {})} | custom-call | tf_op jit(solution)/shard_map/join/pallas_call | solution.py:268
  (15 shorter events, 0.0 us)
Async XLA Ops:
  2.0 25.8 %collective-permute-start.4 = (bf16[2,4,384,128]{3,2,1,0:T(8,128)(2,1)S(1)}, bf16[2,4,384,128]{3,2,1,0:T(8,128)(2,1)S(1)}, u32[]{:S(2)}, u32[]{:S(2)}) collective-permute-start(bf16[2,4,384,128]{3,2,1,0:T(8,128)(2,1)S(1)} %get-tuple-element.37.own), channel_id=1, source_target_pairs={{0,2},{2,0},{4,6},{6,4},{8,10},{10,8},{12,14},{14,12},{16,18},{18,... | collective-permute-start | bytes 2359304 | tf_op jit(solution)/shard_map/ppermute | solution.py:30
  2.6 15.5 %collective-permute-start.8 = (bf16[2,2,384,128]{3,2,1,0:T(8,128)(2,1)S(1)}, bf16[2,2,384,128]{3,2,1,0:T(8,128)(2,1)S(1)}, u32[]{:S(2)}, u32[]{:S(2)}) collective-permute-start(bf16[2,2,384,128]{3,2,1,0:T(8,128)(2,1)S(1)} %get-tuple-element.48), channel_id=1, source_target_pairs={{0,4},{2,6},{4,8},{6,10},{8,12},{10,14},{12,16},{14,18},{16,20},{1... | collective-permute-start | bytes 1179656 | tf_op jit(solution)/shard_map/ppermute | solution.py:26
  5.1 21.2 %collective-permute-start.2 = (bf16[2,2,384,128]{3,2,1,0:T(8,128)(2,1)S(1)}, bf16[2,2,384,128]{3,2,1,0:T(8,128)(2,1)S(1)}, u32[]{:S(2)}, u32[]{:S(2)}) collective-permute-start(bf16[2,2,384,128]{3,2,1,0:T(8,128)(2,1)S(1)} %get-tuple-element.36), channel_id=1, source_target_pairs={{0,4},{2,6},{4,8},{6,10},{8,12},{10,14},{12,16},{14,18},{16,20},{1... | collective-permute-start | bytes 1179656 | tf_op jit(solution)/shard_map/ppermute | solution.py:26
  18.1 10.2 %collective-permute-start.9 = (bf16[2,2,384,128]{3,2,1,0:T(8,128)(2,1)S(1)}, bf16[2,2,384,128]{3,2,1,0:T(8,128)(2,1)S(1)}, u32[]{:S(2)}, u32[]{:S(2)}) collective-permute-start(bf16[2,2,384,128]{3,2,1,0:T(8,128)(2,1)S(1)} %collective-permute-done.8.far), channel_id=1, source_target_pairs={{0,2},{2,0},{4,6},{6,4},{8,10},{10,8},{12,14},{14,12},{16,18},{18,... | collective-permute-start | bytes 1179656 | tf_op jit(solution)/shard_map/ppermute | solution.py:30
  18.1 4.6 %copy-start.1 = (bf16[192,32,128]{2,1,0:T(8,128)(2,1)S(1)}, bf16[192,32,128]{2,1,0:T(8,128)(2,1)}, u32[]{:S(2)}) copy-start(bf16[192,32,128]{2,1,0:T(8,128)(2,1)} %src.2) | copy-start | bytes 4718596
  19.3 3.4 %copy-start = (bf16[192,32,128]{2,1,0:T(8,128)(2,1)S(1)}, bf16[192,32,128]{2,1,0:T(8,128)(2,1)}, u32[]{:S(2)}) copy-start(bf16[192,32,128]{2,1,0:T(8,128)(2,1)} %src.3) | copy-start | bytes 4718596
  19.3 22.7 %collective-permute-start.10 = (bf16[192,8,128]{2,1,0:T(8,128)(2,1)S(1)}, bf16[192,8,128]{2,1,0:T(8,128)(2,1)S(1)}, u32[]{:S(2)}, u32[]{:S(2)}) collective-permute-start(bf16[192,8,128]{2,1,0:T(8,128)(2,1)S(1)} %first.2), channel_id=1, source_target_pairs={{0,1},{1,0},{2,3},{3,2},{4,5},{5,4},{6,7},{7,6},{8,9},{9,8},{10,11... | collective-permute-start | bytes 1179656 | tf_op jit(solution)/shard_map/ppermute | solution.py:30
  22.2 1.4 %copy-start.2 = (bf16[192,32,128]{2,1,0:T(8,128)(2,1)S(1)}, bf16[192,32,128]{2,1,0:T(8,128)(2,1)}, u32[]{:S(2)}) copy-start(bf16[192,32,128]{2,1,0:T(8,128)(2,1)} %o.1) | copy-start | bytes 4718596
  22.2 1.4 %copy-start.3 = (f32[192,32]{0,1:T(8,128)S(1)}, f32[192,32]{0,1:T(8,128)}, u32[]{:S(2)}) copy-start(f32[192,32]{0,1:T(8,128)} %param.11) | copy-start | bytes 73732
  22.2 19.8 %collective-permute-start.11 = (bf16[192,8,128]{2,1,0:T(8,128)(2,1)S(1)}, bf16[192,8,128]{2,1,0:T(8,128)(2,1)S(1)}, u32[]{:S(2)}, u32[]{:S(2)}) collective-permute-start(bf16[192,8,128]{2,1,0:T(8,128)(2,1)S(1)} %first.3), channel_id=1, source_target_pairs={{0,1},{1,0},{2,3},{3,2},{4,5},{5,4},{6,7},{7,6},{8,9},{9,8},{10,11... | collective-permute-start | bytes 1179656 | tf_op jit(solution)/shard_map/ppermute | solution.py:30
  26.3 14.0 %collective-permute-start.1 = (f32[2,4,768]{2,1,0:T(4,128)S(1)}, f32[2,4,768]{2,1,0:T(4,128)S(1)}, u32[]{:S(2)}, u32[]{:S(2)}) collective-permute-start(f32[2,4,768]{2,1,0:T(4,128)S(1)} %get-tuple-element.35), channel_id=1, source_target_pairs={{0,1},{1,0},{2,3},{3,2},{4,5},{5,4},{6,7},{7,6},{8,9},{9,8},{10,11... | collective-permute-start | bytes 73736 | tf_op jit(solution)/shard_map/ppermute | solution.py:30
  27.8 22.7 %collective-permute-start = (bf16[2,768,128]{2,1,0:T(8,128)(2,1)S(1)}, bf16[2,768,128]{2,1,0:T(8,128)(2,1)S(1)}, u32[]{:S(2)}, u32[]{:S(2)}) collective-permute-start(bf16[2,768,128]{2,1,0:T(8,128)(2,1)S(1)} %get-tuple-element.34), channel_id=1, source_target_pairs={{0,1},{1,0},{2,3},{3,2},{4,5},{5,4},{6,7},{7,6},{8,9},{9,8},{10,11... | collective-permute-start | bytes 1179656 | tf_op jit(solution)/shard_map/ppermute | solution.py:30
  28.3 18.1 %collective-permute-start.3 = (bf16[2,2,384,128]{3,2,1,0:T(8,128)(2,1)S(1)}, bf16[2,2,384,128]{3,2,1,0:T(8,128)(2,1)S(1)}, u32[]{:S(2)}, u32[]{:S(2)}) collective-permute-start(bf16[2,2,384,128]{3,2,1,0:T(8,128)(2,1)S(1)} %collective-permute-done.2.far), channel_id=1, source_target_pairs={{0,2},{2,0},{4,6},{6,4},{8,10},{10,8},{12,14},{14,12},{16,18},{18,... | collective-permute-start | bytes 1179656 | tf_op jit(solution)/shard_map/ppermute | solution.py:30
  40.3 16.9 %collective-permute-start.6 = (bf16[2,768,128]{2,1,0:T(8,128)(2,1)S(1)}, bf16[2,768,128]{2,1,0:T(8,128)(2,1)S(1)}, u32[]{:S(2)}, u32[]{:S(2)}) collective-permute-start(bf16[2,768,128]{2,1,0:T(8,128)(2,1)S(1)} %get-tuple-element.43), channel_id=1, source_target_pairs={{0,1},{1,0},{2,3},{3,2},{4,5},{5,4},{6,7},{7,6},{8,9},{9,8},{10,11... | collective-permute-start | bytes 1179656 | tf_op jit(solution)/shard_map/ppermute | solution.py:30
  46.0 13.2 %collective-permute-start.15 = (bf16[2,2,384,128]{3,2,1,0:T(8,128)(2,1)S(1)}, bf16[2,2,384,128]{3,2,1,0:T(8,128)(2,1)S(1)}, u32[]{:S(2)}, u32[]{:S(2)}) collective-permute-start(bf16[2,2,384,128]{3,2,1,0:T(8,128)(2,1)S(1)} %get-tuple-element.59), channel_id=1, source_target_pairs={{0,2},{2,0},{4,6},{6,4},{8,10},{10,8},{12,14},{14,12},{16,18},{18,... | collective-permute-start | bytes 1179656 | tf_op jit(solution)/shard_map/ppermute | solution.py:30
  46.1 19.5 %collective-permute-start.12 = (bf16[2,768,128]{2,1,0:T(8,128)(2,1)S(1)}, bf16[2,768,128]{2,1,0:T(8,128)(2,1)S(1)}, u32[]{:S(2)}, u32[]{:S(2)}) collective-permute-start(bf16[2,768,128]{2,1,0:T(8,128)(2,1)S(1)} %get-tuple-element.53), channel_id=1, source_target_pairs={{0,1},{1,0},{2,3},{3,2},{4,5},{5,4},{6,7},{7,6},{8,9},{9,8},{10,11... | collective-permute-start | bytes 1179656 | tf_op jit(solution)/shard_map/ppermute | solution.py:30
  52.5 10.4 %collective-permute-start.16 = (bf16[2,1,384,128]{3,2,1,0:T(8,128)(2,1)S(1)}, bf16[2,1,384,128]{3,2,1,0:T(8,128)(2,1)S(1)}, u32[]{:S(2)}, u32[]{:S(2)}) collective-permute-start(bf16[2,1,384,128]{3,2,1,0:T(8,128)(2,1)S(1)} %get-tuple-element.60), channel_id=1, source_target_pairs={{0,2},{2,0},{4,6},{6,4},{8,10},{10,8},{12,14},{14,12},{16,18},{18,... | collective-permute-start | bytes 589832 | tf_op jit(solution)/shard_map/ppermute | solution.py:30
  59.1 4.3 %collective-permute-start.13 = (bf16[2,1,384,128]{3,2,1,0:T(8,128)(2,1)S(1)}, bf16[2,1,384,128]{3,2,1,0:T(8,128)(2,1)S(1)}, u32[]{:S(2)}, u32[]{:S(2)}) collective-permute-start(bf16[2,1,384,128]{3,2,1,0:T(8,128)(2,1)S(1)} %get-tuple-element.55), channel_id=1, source_target_pairs={{0,2},{2,0},{4,6},{6,4},{8,10},{10,8},{12,14},{14,12},{16,18},{18,... | collective-permute-start | bytes 589832 | tf_op jit(solution)/shard_map/ppermute | solution.py:30
  59.3 16.3 %collective-permute-start.17 = (bf16[2,2,384,128]{3,2,1,0:T(8,128)(2,1)S(1)}, bf16[2,2,384,128]{3,2,1,0:T(8,128)(2,1)S(1)}, u32[]{:S(2)}, u32[]{:S(2)}) collective-permute-start(bf16[2,2,384,128]{3,2,1,0:T(8,128)(2,1)S(1)} %merge.4), channel_id=1, source_target_pairs={{0,28},{2,30},{4,0},{6,2},{8,4},{10,6},{12,8},{14,10},{16,12},{18,... | collective-permute-start | bytes 1179656 | tf_op jit(solution)/shard_map/ppermute | solution.py:26
  61.4 8.4 %collective-permute-start.7 = (bf16[1,768,128]{2,1,0:T(8,128)(2,1)S(1)}, bf16[1,768,128]{2,1,0:T(8,128)(2,1)S(1)}, u32[]{:S(2)}, u32[]{:S(2)}) collective-permute-start(bf16[1,768,128]{2,1,0:T(8,128)(2,1)S(1)} %get-tuple-element.45), channel_id=1, source_target_pairs={{0,1},{1,0},{2,3},{3,2},{4,5},{5,4},{6,7},{7,6},{8,9},{9,8},{10,11... | collective-permute-start | bytes 589832 | tf_op jit(solution)/shard_map/ppermute | solution.py:30
  62.9 10.7 %collective-permute-start.5 = (bf16[1,768,128]{2,1,0:T(8,128)(2,1)S(1)}, bf16[1,768,128]{2,1,0:T(8,128)(2,1)S(1)}, u32[]{:S(2)}, u32[]{:S(2)}) collective-permute-start(bf16[1,768,128]{2,1,0:T(8,128)(2,1)S(1)} %get-tuple-element.42), channel_id=1, source_target_pairs={{0,1},{1,0},{2,3},{3,2},{4,5},{5,4},{6,7},{7,6},{8,9},{9,8},{10,11... | collective-permute-start | bytes 589832 | tf_op jit(solution)/shard_map/ppermute | solution.py:30
  63.5 12.1 %collective-permute-start.18 = (bf16[2,1,384,128]{3,2,1,0:T(8,128)(2,1)S(1)}, bf16[2,1,384,128]{3,2,1,0:T(8,128)(2,1)S(1)}, u32[]{:S(2)}, u32[]{:S(2)}) collective-permute-start(bf16[2,1,384,128]{3,2,1,0:T(8,128)(2,1)S(1)} %merge.5), channel_id=1, source_target_pairs={{0,28},{2,30},{4,0},{6,2},{8,4},{10,6},{12,8},{14,10},{16,12},{18,... | collective-permute-start | bytes 589832 | tf_op jit(solution)/shard_map/ppermute | solution.py:26
  65.6 13.7 %collective-permute-start.14 = (bf16[2,1,384,128]{3,2,1,0:T(8,128)(2,1)S(1)}, bf16[2,1,384,128]{3,2,1,0:T(8,128)(2,1)S(1)}, u32[]{:S(2)}, u32[]{:S(2)}) collective-permute-start(bf16[2,1,384,128]{3,2,1,0:T(8,128)(2,1)S(1)} %merge.3), channel_id=1, source_target_pairs={{0,28},{2,30},{4,0},{6,2},{8,4},{10,6},{12,8},{14,10},{16,12},{18,... | collective-permute-start | bytes 589832 | tf_op jit(solution)/shard_map/ppermute | solution.py:26
